TPU v7x, 32 devices: a whole 2x2x4 slice. The times are simulated.
32 devices in a mesh: pairs: 8 (over z, x), win: 4 (over y, core).
Axes of the slice: x: 2, y: 2, z: 4, core: 2. Of those that a mesh axis runs over, the one named last changes fastest.
Arguments:
- spectra: float32 [128, 8, 2, 3200], P('pairs', 'win'), as said below
- requests: int32 [8, 8, 8], P('pairs'), may hold values from -1 to 15, as said below
- pair_first: int32 [4096], P('pairs'), may hold values from 0 to 63, as said below
- pair_second: int32 [4096], P('pairs'), may hold values from 0 to 63, as said below
Outputs:
- stacks: float32 [2048, 4096], P('win', 'pairs')
Inputs may be any that keep to these rules, and one draw needn't show every extreme that they name: requests[o, s, c] is a row of source device s's 16 stations that owner o needs, or -1 for an empty slot; an owner's rows from one source are distinct and fill the slots from 0 onward; every owner takes 8 rows from some source. `pair_first`: pair p belongs to owner p // 512 and names one of that owner's 8 x 8 slots, source-major, never an empty one. `pair_second`: as pair_first. Finite band spectra.
All inputs are finite; a program needn't handle non-finite values.
Results may differ from a plain program's by a relative error of at most 0.01.
Values may be sent and summed in bfloat16 or wider, within the bound.
No kernel may reach another device: no remote copies, remote signals or barrier semaphores. Data moves between devices by JAX's collectives and lax.ppermute only.
A program may use at most 128 MiB of HBM per device.

v0:
```python
import functools
import math

import jax
import jax.numpy as jnp
from jax import lax
from jax.experimental import pallas as pl
from jax.experimental.pallas import tpu as pltpu
from jax.sharding import PartitionSpec as P


LAGS = 2048
NFFT = 18000
K0 = 360
LANES = 128
EPS = 1e-06
FINE = 32
VMEM = pl.BlockSpec(memory_space=pltpu.VMEM)
SMEM = pl.BlockSpec(memory_space=pltpu.SMEM)


def params(*nbytes, roomy=False):
    limit = 60 if roomy else sum(nbytes) // 1024**2 + 5
    return pltpu.CompilerParams(vmem_limit_bytes=limit * 1024**2)


def size(shape, dtype):
    return math.prod(shape) * jnp.dtype(dtype).itemsize


def whiten_kernel(core_ref, raw_ref, keep_big, keep_small, give_big, give_small, tmp):
    stations, windows, _, bins = raw_ref.shape
    blocks = bins // LANES
    half = blocks // 2
    core = core_ref[0]

    def white(re, im):
        power = jnp.sum(re * re + im * im, axis=1, keepdims=True) * (1.0 / (2 * LANES))
        scale = lax.rsqrt(power + EPS)
        return re * scale, im * scale

    def station(s, slot):
        for w in range(windows):
            for b in range(blocks):
                value = raw_ref[s, w, :, b * LANES : (b + 1) * LANES]
                side, at = divmod(b, half)
                if side == 2:
                    row = 96 + w
                elif at < 8:
                    row = side * 48 + w * 16 + at
                else:
                    row = side * 48 + 32 + w * 4 + at - 8
                tmp[slot, pl.ds(row, 2, stride=8), :] = value
        for mine, big, small in ((True, keep_big, keep_small), (False, give_big, give_small)):
            base = pl.multiple_of((core if mine else 1 - core) * 48, 16)
            for g in range(3):
                re = tmp[slot, pl.ds(base + g * 16, 8), :]
                im = tmp[slot, pl.ds(base + g * 16 + 8, 8), :]
                rows = jnp.concatenate(white(re, im), axis=0).astype(jnp.bfloat16)
                if g < 2:
                    big[s, g * 16 : g * 16 + 16, :] = rows
                else:
                    small[s, 0:16, :] = rows
        re, im = white(tmp[slot, 96:104, :], tmp[slot, 104:112, :])
        tmp[slot, 112:114, :] = re[0:windows]
        tmp[slot, 114:116, :] = im[0:windows]
        keep_small[s, 16:24, :] = tmp[slot, 112:120, :].astype(jnp.bfloat16)

    tmp[...] = jnp.zeros_like(tmp)

    def several(i, carry):
        for slot in range(2):
            station(2 * i + slot, slot)
        return carry

    lax.fori_loop(0, stations // 2, several, 0)


def whiten(core, raw):
    stations = raw.shape[0]
    rows = (32, 24, 32, 16)
    return pl.pallas_call(
        whiten_kernel,
        name="whiten",
        out_shape=tuple(jax.ShapeDtypeStruct((stations, r, LANES), jnp.bfloat16) for r in rows),
        in_specs=[SMEM, VMEM],
        out_specs=(VMEM,) * 4,
        scratch_shapes=[pltpu.VMEM((2, 120, LANES), jnp.float32)],
        compiler_params=params(2 * size(raw.shape, raw.dtype)),
        cost_estimate=pl.CostEstimate(flops=2_000_000, bytes_accessed=2_000_000, transcendentals=0),
    )(core, raw)


def join(keep, got, small):
    if small:
        return jnp.concatenate([keep[:, :16], got, keep[:, 16:]], axis=1)
    return jnp.concatenate([keep, got], axis=1)


def select_kernel(peers, sources, cap, small, me_ref, *refs):
    asked = refs[:peers]
    chunks = refs[peers : peers + 4]
    outs = refs[peers + 4 :]
    me = me_ref[0]
    for d in range(peers):
        for h in range(2):
            source = me ^ (h * (sources // 2))
            keep, got = chunks[2 * h : 2 * h + 2]
            for c in range(cap):
                row = jnp.maximum(asked[d][source, c], 0)
                out = outs[d].at[h * cap + c]
                if small:
                    out[0:16] = keep[row, 0:16]
                    out[16:32] = got[row]
                    out[32:40] = keep[row, 16:24]
                else:
                    out[0:32] = keep[row]
                    out[32:64] = got[row]


def select(me, asked, chunks, cap, small):
    peers = len(asked)
    sources = asked[0].shape[0]
    rows = chunks[0].shape[1] + chunks[1].shape[1]
    out = jax.ShapeDtypeStruct((2 * cap, rows, LANES), chunks[0].dtype)
    return pl.pallas_call(
        functools.partial(select_kernel, peers, sources, cap, small),
        name="select",
        out_shape=(out,) * peers,
        in_specs=[SMEM] * (1 + peers) + [VMEM] * 4,
        out_specs=(VMEM,) * peers,
        compiler_params=params(2 * (peers + 2) * size(out.shape, out.dtype)),
        cost_estimate=pl.CostEstimate(flops=0, bytes_accessed=1_000_000, transcendentals=0),
    )(me, *asked, *chunks)


def load_table(bufs, table):
    at = 0
    for buf in bufs:

        def copy(i, carry, buf=buf, at=at):
            table[at + i] = buf[i].astype(jnp.float32)
            return carry

        lax.fori_loop(0, buf.shape[0], copy, 0, unroll=4)
        at += buf.shape[0]


def products(table, i, j, groups):
    re = im = None
    for g in range(groups):
        ar = table[i, g * 16 : g * 16 + 8, :]
        ai = table[i, g * 16 + 8 : g * 16 + 16, :]
        br = table[j, g * 16 : g * 16 + 8, :]
        bi = table[j, g * 16 + 8 : g * 16 + 16, :]
        r = ar * br + ai * bi
        m = ai * br - ar * bi
        re = r if re is None else re + r
        im = m if im is None else im + m
    return re, im


BIG_ROWS = 17
SMALL_ROWS = 25


def cross_big(first_ref, second_ref, bufs, table, cross, out):
    pairs = out.shape[0]
    load_table(bufs, table)

    def pair(p, carry):
        re, im = products(table, first_ref[p], second_ref[p], 4)
        cross[pl.ds(p * BIG_ROWS, 8), :] = re
        cross[pl.ds(p * BIG_ROWS + 8, 8), :] = im
        return carry

    lax.fori_loop(0, pairs, pair, 0, unroll=8)
    for k in range(16):
        out[:, k * LANES : (k + 1) * LANES] = cross[pl.ds(k, pairs, stride=BIG_ROWS), :].astype(
            jnp.bfloat16
        )


def cross_small(first_ref, second_ref, bufs, table, cross, out):
    pairs = out.shape[0]
    load_table(bufs, table)

    def pair(p, carry):
        i = first_ref[p]
        j = second_ref[p]
        re, im = products(table, i, j, 2)
        at = p * SMALL_ROWS
        cross[pl.ds(at, 8), :] = re
        cross[pl.ds(at + 8, 8), :] = im
        a = table[i, 32:40, :]
        b = table[j, 32:40, :]
        cross[pl.ds(at + 16, 2), :] = a[0:2] * b[0:2] + a[2:4] * b[2:4]
        cross[pl.ds(at + 18, 2), :] = a[2:4] * b[0:2] - a[0:2] * b[2:4]
        return carry

    lax.fori_loop(0, pairs, pair, 0, unroll=8)

    def column(row):
        return cross[pl.ds(row, pairs, stride=SMALL_ROWS), :]

    for k in range(8):
        row = (k // 4) * 8 + k % 4
        out[:, k * LANES : (k + 1) * LANES] = (column(row) + column(row + 4)).astype(jnp.bfloat16)
    for k in range(2):
        row = 16 + 2 * k
        out[:, (8 + k) * LANES : (9 + k) * LANES] = (column(row) + column(row + 1)).astype(
            jnp.bfloat16
        )


def table_kernel(coarse_ref, fine_ref, big_ref, small_ref):
    half = fine_ref.shape[2] // LANES - 1
    for g in range(half + 1):
        at = slice(g * LANES, (g + 1) * LANES)
        cf = fine_ref[0, :, at]
        sf = fine_ref[1, :, at]
        if g < 8:
            ref, re, im = big_ref, g, g + 8
        elif g < half:
            ref, re, im = small_ref, g - 8, g - 8 + half - 8
        else:
            ref, re, im = small_ref, 2 * (half - 8), 2 * (half - 8) + 1
        for u in range(coarse_ref.shape[1]):
            cc = coarse_ref[0, u : u + 1, at]
            sc = coarse_ref[1, u : u + 1, at]
            rows = slice(u * FINE, (u + 1) * FINE)
            ref[rows, re * LANES : (re + 1) * LANES] = (cc * cf - sc * sf).astype(jnp.bfloat16)
            ref[rows, im * LANES : (im + 1) * LANES] = (sc * cf + cc * sf).astype(jnp.bfloat16)


def lag_bases(core, half, blocks):
    block_index = jnp.concatenate(
        [core * half + jnp.arange(half, dtype=jnp.int32), jnp.full((1,), blocks - 1, jnp.int32)]
    )
    bins = (K0 + block_index[:, None] * LANES + jnp.arange(LANES, dtype=jnp.int32)).reshape(-1)

    def base(lags):
        angles = (lags[:, None] * bins[None, :] % NFFT).astype(jnp.float32) * (2.0 * math.pi / NFFT)
        return jnp.stack([jnp.cos(angles), -jnp.sin(angles)])

    coarse = base(jnp.arange(LAGS // FINE, dtype=jnp.int32) * FINE - LAGS // 2)
    fine = base(jnp.arange(FINE, dtype=jnp.int32))
    return coarse, fine


def lag_table(coarse, fine):
    width = fine.shape[2]
    half = width // LANES - 1
    step = 8
    return pl.pallas_call(
        table_kernel,
        name="lagtable",
        grid=(LAGS // FINE // step,),
        out_shape=(
            jax.ShapeDtypeStruct((LAGS, 16 * LANES), jnp.bfloat16),
            jax.ShapeDtypeStruct((LAGS, 2 * (half + 1 - 8) * LANES), jnp.bfloat16),
        ),
        in_specs=[
            pl.BlockSpec((2, step, width), lambda u: (0, u, 0)),
            pl.BlockSpec((2, FINE, width), lambda u: (0, 0, 0)),
        ],
        out_specs=(
            pl.BlockSpec((step * FINE, 16 * LANES), lambda u: (u, 0)),
            pl.BlockSpec((step * FINE, 2 * (half + 1 - 8) * LANES), lambda u: (u, 0)),
        ),
        compiler_params=params(),
        cost_estimate=pl.CostEstimate(
            flops=LAGS * width * 6, bytes_accessed=LAGS * width * 4, transcendentals=0
        ),
    )(coarse, fine)


def dot_nt(a, b):
    return lax.dot_general(a, b, (((1,), (1,)), ((), ())), preferred_element_type=jnp.float32)


def stack_big_kernel(count, tile, first_ref, second_ref, *refs):
    bufs = refs[:count]
    lag_ref, acc_ref, table, rows, cross = refs[count:]
    cross_big(first_ref, second_ref, bufs, table, rows, cross)
    for t in range(acc_ref.shape[0] // tile):
        at = slice(t * tile, (t + 1) * tile)
        acc_ref[at, :] = dot_nt(lag_ref[at, :], cross[...])


def stack_big(first, second, bufs, lag_table, tile):
    lags, depth = lag_table.shape
    pairs = first.shape[0]
    slots = sum(buf.shape[0] for buf in bufs)
    table = ((slots,) + bufs[0].shape[1:], jnp.float32)
    rows = ((pairs * BIG_ROWS, LANES), jnp.float32)
    cross = ((pairs, depth), jnp.bfloat16)
    return pl.pallas_call(
        functools.partial(stack_big_kernel, len(bufs), tile),
        name="stack0",
        out_shape=jax.ShapeDtypeStruct((lags, pairs), jnp.float32),
        in_specs=[SMEM, SMEM] + [VMEM] * (len(bufs) + 1),
        out_specs=VMEM,
        scratch_shapes=[pltpu.VMEM(*table), pltpu.VMEM(*rows), pltpu.VMEM(*cross)],
        compiler_params=params(size(*table), size(*rows), size(*cross), roomy=len(bufs) == 1),
        cost_estimate=pl.CostEstimate(
            flops=2 * lags * depth * pairs,
            bytes_accessed=2 * lags * depth + 4 * lags * pairs,
            transcendentals=0,
        ),
    )(first, second, *bufs, lag_table)


def finish(part, core, lag_ref, acc_ref, cross, send_ref, keep_ref):
    outer, tile, _ = send_ref.shape
    group_rows = lag_ref.shape[0] // (2 * outer)
    for mine in range(2):
        for at in range(outer):
            group = 2 * at + (core if mine else 1 - core)
            rows = pl.ds(pl.multiple_of(group * group_rows + part * tile, tile), tile)
            value = acc_ref[rows, :] + dot_nt(lag_ref[rows, :], cross[...])
            if mine:
                keep_ref[at] = value
            else:
                send_ref[at] = value.astype(send_ref.dtype)


def stack_first_kernel(count, core_ref, first_ref, second_ref, *refs):
    bufs = refs[:count]
    lag_ref, acc_ref, send_ref, keep_ref, cross, table, rows = refs[count:]
    cross_small(first_ref, second_ref, bufs, table, rows, cross)
    finish(0, core_ref[0], lag_ref, acc_ref, cross, send_ref, keep_ref)


def stack_next_kernel(part, core_ref, lag_ref, acc_ref, cross, send_ref, keep_ref):
    finish(part, core_ref[0], lag_ref, acc_ref, cross, send_ref, keep_ref)


def stack_outputs(acc, groups, parts):
    lags, pairs = acc.shape
    shape = (groups // 2, lags // groups // parts, pairs)
    return [jax.ShapeDtypeStruct(shape, jnp.bfloat16), jax.ShapeDtypeStruct(shape, jnp.float32)]


def stack_cost(lags, depth, pairs, parts):
    return pl.CostEstimate(
        flops=2 * lags * depth * pairs // parts,
        bytes_accessed=(2 * lags * depth + 8 * lags * pairs) // parts,
        transcendentals=0,
    )


def stack_first(core, first, second, bufs, lag_table, acc, groups, parts):
    lags, depth = lag_table.shape
    pairs = acc.shape[1]
    slots = sum(buf.shape[0] for buf in bufs)
    table = ((slots,) + bufs[0].shape[1:], jnp.float32)
    rows = ((pairs * SMALL_ROWS, LANES), jnp.float32)
    return pl.pallas_call(
        functools.partial(stack_first_kernel, len(bufs)),
        name="stack1",
        in_specs=[SMEM] * 3 + [VMEM] * (len(bufs) + 2),
        out_specs=[VMEM] * 3,
        scratch_shapes=[pltpu.VMEM(*table), pltpu.VMEM(*rows)],
        out_shape=stack_outputs(acc, groups, parts)
        + [jax.ShapeDtypeStruct((pairs, depth), jnp.bfloat16)],
        compiler_params=params(size(*table), size(*rows), roomy=len(bufs) == 1),
        cost_estimate=stack_cost(lags, depth, pairs, parts),
    )(core, first, second, *bufs, lag_table, acc)


def stack_next(core, lag_table, acc, cross, groups, part, parts):
    lags, depth = lag_table.shape
    return pl.pallas_call(
        functools.partial(stack_next_kernel, part),
        name="stack2",
        in_specs=[SMEM] + [VMEM] * 3,
        out_specs=[VMEM] * 2,
        out_shape=stack_outputs(acc, groups, parts),
        compiler_params=params(),
        cost_estimate=stack_cost(lags, depth, acc.shape[1], parts),
    )(core, lag_table, acc, cross)


def away_kernel(place_ref, keep_ref, near_ref, *outs):
    for d, out in enumerate(outs):
        at = place_ref[0] ^ (d + 1)
        out[...] = (keep_ref[at] + near_ref[at].astype(jnp.float32)).astype(out.dtype)


def sum_away(place, keep, near):
    outer, lags, pairs = keep.shape
    return pl.pallas_call(
        away_kernel,
        name="away",
        out_shape=[jax.ShapeDtypeStruct((lags, pairs), near.dtype)] * (outer - 1),
        in_specs=[SMEM, VMEM, VMEM],
        out_specs=[VMEM] * (outer - 1),
        compiler_params=params(2 * size(keep.shape, jnp.float32)),
        cost_estimate=pl.CostEstimate(
            flops=keep.size, bytes_accessed=6 * keep.size, transcendentals=0
        ),
    )(place, keep, near)


def result_kernel(scale, parts, place_ref, *refs):
    out = refs[-1]
    each = (len(refs) - 1) // parts
    place = place_ref[0]
    for part in range(parts):
        keep, near, *far = refs[part * each : (part + 1) * each]
        total = keep[place] + near[place].astype(jnp.float32)
        for ref in far:
            total = total + ref[...].astype(jnp.float32)
        lags = total.shape[0]
        out[part * lags : (part + 1) * lags, :] = scale * total


def result(place, pieces, scale):
    operands = [x for piece in pieces for x in piece]
    _, lags, pairs = pieces[0][0].shape
    return pl.pallas_call(
        functools.partial(result_kernel, scale, len(pieces)),
        name="result",
        out_shape=jax.ShapeDtypeStruct((lags * len(pieces), pairs), jnp.float32),
        in_specs=[SMEM] + [VMEM] * len(operands),
        out_specs=VMEM,
        compiler_params=params(2 * size((lags * len(pieces), pairs), jnp.float32)),
        cost_estimate=pl.CostEstimate(
            flops=lags * pairs * 4, bytes_accessed=lags * pairs * 16, transcendentals=0
        ),
    )(place, *operands)


def swap(x, axis, mask):
    return lax.ppermute(x, axis, [(i, i ^ mask) for i in range(lax.axis_size(axis))])


def swap_both(x, mask_pairs, mask_win):
    groups = lax.axis_size("win")
    perm = [
        (p * groups + w, (p ^ mask_pairs) * groups + (w ^ mask_win))
        for p in range(lax.axis_size("pairs"))
        for w in range(groups)
    ]
    return lax.ppermute(x, ("pairs", "win"), perm)


def after(x, *earlier):
    return lax.optimization_barrier((x,) + earlier)[0]


def local(spectra, requests, pair_first, pair_second):
    _, windows, _, bins = spectra.shape
    sources = lax.axis_size("pairs")
    groups = lax.axis_size("win")
    cap = requests.shape[2]
    me = lax.axis_index("pairs").astype(jnp.int32)
    group = lax.axis_index("win").astype(jnp.int32)
    core = group & 1
    blocks = bins // LANES
    half = blocks // 2
    assert windows == 2 and blocks == 2 * half + 1 and half == 12 and groups % 2 == 0

    keep_big, keep_small, give_big, give_small = whiten(core[None], spectra)
    coarse, fine = lag_bases(core, half, blocks)
    table_big, table_small = lag_table(coarse, fine)

    slots = sources * cap
    exchange = []
    if two_stage(sources):
        far = sources // 2
        big = [
            keep_big,
            swap(give_big, "win", 1),
            swap(keep_big, "pairs", far),
            swap_both(give_big, far, 1),
        ]
        wanted = after(requests[0], keep_big)
        asked = [wanted] + [swap(wanted, "pairs", d) for d in range(1, far)]
        keep_small = after(keep_small, coarse)
        give_small = after(give_small, coarse)
        small = [
            keep_small,
            swap(give_small, "win", 1),
            swap(keep_small, "pairs", far),
            swap_both(give_small, far, 1),
        ]
        for chunks, name in ((big, "big"), (small, "small")):
            outs = select(me[None], asked, chunks, cap, name == "small")
            exchange.append([outs[0]] + [swap(outs[d], "pairs", d) for d in range(1, far)])

        def row_of(slot):
            apart = (slot // cap) ^ me
            return (apart % far) * (2 * cap) + (apart // far) * cap + slot % cap

    else:
        asked_rows = lax.all_to_all(requests[0], "pairs", split_axis=0, concat_axis=0, tiled=True)
        for i, (keep, give) in enumerate(((keep_big, give_big), (keep_small, give_small))):
            chunk = join(keep, swap(give, "win", 1), i == 1)
            outgoing = chunk[jnp.maximum(asked_rows, 0)]
            arrived = lax.all_to_all(outgoing, "pairs", split_axis=0, concat_axis=0, tiled=True)
            exchange.append([arrived.reshape((slots,) + chunk.shape[1:])])

        def row_of(slot):
            return slot

    first = row_of(pair_first)
    second = row_of(pair_second)
    acc = stack_big(first, second, exchange[0], table_big, LAGS // groups)

    place = (group >> 1)[None]
    parts = 2
    pieces = []
    send, keep, cross = stack_first(
        core[None], first, second, exchange[1], table_small, acc, groups, parts
    )
    for part in range(parts):
        if part > 0:
            send, keep = stack_next(core[None], table_small, acc, cross, groups, part, parts)
        near = swap(send, "win", 1)
        away = sum_away(place, keep, near)
        pieces.append([keep, near] + [swap(x, "win", 2 * (d + 1)) for d, x in enumerate(away)])
    return result(place, pieces, 1.0 / math.sqrt(bins * windows * groups))


def two_stage(sources):
    return sources & (sources - 1) == 0 and 4 <= sources <= 16


def solution(mesh):
    return jax.shard_map(
        local,
        mesh=mesh,
        in_specs=(P("pairs", "win", None, None), P("pairs", None, None), P("pairs"), P("pairs")),
        out_specs=P("win", "pairs"),
        check_vma=False,
    )
```

profile of v0, /device:TPU:0, one launch (start us, length us, event | category | flops | bytes accessed | tf_op | source)
XLA Modules:
  0.0 79.3 jit_solution(11454509599765088917)
XLA Ops:
  0.0 1.2 %copy-done = f32[16,2,2,3200]{3,2,1,0:T(2,128)S(1)} copy-done((f32[16,2,2,3200]{3,2,1,0:T(2,128)S(1)}, f32[16,2,2,3200]{3,2,1,0:T(2,128)}, u32[]{:S(2)}) %copy-start) | copy-done | bytes 819224
  1.2 1.6 %whiten.1 = (bf16[16,32,128]{2,1,0:T(8,128)(2,1)S(1)}, bf16[16,24,128]{2,1,0:T(8,128)(2,1)S(1)}, bf16[16,32,128]{2,1,0:T(8,128)(2,1)S(1)}, bf16[16,16,128]{2,1,0:T(8,128)(2,1)S(1)}) custom-call(s32[1]{0:T(128)} %bitcast.1.core_ref, f32[16,2,2,3200]{3,2,1,0:T(2,128)S(1)} %copy-done), custom_call_target="tpu_custom_call" | custom-call | flops 2000000 | bytes 2000000 | tf_op jit(solution)/shard_map/whiten/pallas_call | solution.py:82
  2.8 4.0 %collective-permute-start.2 = (s32[8,8]{1,0:T(8,128)}, s32[8,8]{1,0:T(8,128)S(1)}, u32[]{:S(2)}, u32[]{:S(2)}) collective-permute-start(s32[8,8]{1,0:T(8,128)} %bitcast.6), channel_id=1, source_target_pairs={{0,12},{4,8},{8,4},{12,0},{16,28},{20,24},{24,20},{28,16},{1,13},{... | collective-permute-start | bytes 776 | tf_op jit(solution)/shard_map/ppermute | solution.py:436
  6.9 0.4 collective-permute-start.1
  7.3 1.5 %collective-permute-start.11 = (bf16[16,32,128]{2,1,0:T(8,128)(2,1)S(1)}, bf16[16,32,128]{2,1,0:T(8,128)(2,1)S(1)}, u32[]{:S(2)}, u32[]{:S(2)}) collective-permute-start(bf16[16,32,128]{2,1,0:T(8,128)(2,1)S(1)} %get-tuple-element.38), channel_id=1, source_target_pairs={{0,17},{1,16},{2,19},{3,18},{4,21},{5,20},{6,23},{7,22},{8,25},{9,... | collective-permute-start | bytes 393224 | tf_op jit(solution)/shard_map/ppermute | solution.py:446
  8.8 1.2 %collective-permute-start.9 = (bf16[16,32,128]{2,1,0:T(8,128)(2,1)S(1)}, bf16[16,32,128]{2,1,0:T(8,128)(2,1)S(1)}, u32[]{:S(2)}, u32[]{:S(2)}) collective-permute-start(bf16[16,32,128]{2,1,0:T(8,128)(2,1)S(1)} %get-tuple-element.38), channel_id=1, source_target_pairs={{0,1},{1,0},{2,3},{3,2},{4,5},{5,4},{6,7},{7,6},{8,9},{9,8},{10,11... | collective-permute-start | bytes 393224 | tf_op jit(solution)/shard_map/ppermute | solution.py:436
  10.5 0.9 %fusion.10 = (f32[1,32,1664]{2,1,0:T(8,128)S(1)}, f32[1,32,1664]{2,1,0:T(8,128)S(1)}) fusion(s32[1664]{0:T(1024)S(1)} %add_bitcast_fusion), kind=kLoop, calls=%fused_computation.18 | loop fusion | flops 532480 | bytes 432640 | tf_op jit(solution)/shard_map/cos | solution.py:244
  11.4 1.8 %fusion.4 = (f32[1,64,1664]{2,1,0:T(8,128)S(1)}, f32[1,64,1664]{2,1,0:T(8,128)S(1)}) fusion(s32[1664]{0:T(1024)S(1)} %add_bitcast_fusion, s32[64]{0:T(128)S(1)} %multiply_add_fusion), kind=kLoop, calls=%fused_computation.9 | loop fusion | flops 1064960 | bytes 858880 | tf_op jit(solution)/shard_map/cos | solution.py:244
  13.6 2.0 %collective-permute-start.5 = (bf16[16,16,128]{2,1,0:T(8,128)(2,1)S(1)}, bf16[16,16,128]{2,1,0:T(8,128)(2,1)S(1)}, u32[]{:S(2)}, u32[]{:S(2)}) collective-permute-start(bf16[16,16,128]{2,1,0:T(8,128)(2,1)S(1)} %get-tuple-element.32), channel_id=1, source_target_pairs={{0,17},{1,16},{2,19},{3,18},{4,21},{5,20},{6,23},{7,22},{8,25},{9,... | collective-permute-start | bytes 196616 | tf_op jit(solution)/shard_map/ppermute | solution.py:446
  15.5 1.6 %collective-permute-done.refs_1_ = s32[8,8]{1,0:T(8,128)S(1)} collective-permute-done((s32[8,8]{1,0:T(8,128)}, s32[8,8]{1,0:T(8,128)S(1)}, u32[]{:S(2)}, u32[]{:S(2)}) %collective-permute-start) | collective-permute-done | bytes 288 | tf_op jit(solution)/shard_map/ppermute | solution.py:436
  17.2 3.6 %collective-permute-done.11.refs_7_ = bf16[16,32,128]{2,1,0:T(8,128)(2,1)S(1)} collective-permute-done((bf16[16,32,128]{2,1,0:T(8,128)(2,1)S(1)}, bf16[16,32,128]{2,1,0:T(8,128)(2,1)S(1)}, u32[]{:S(2)}, u32[]{:S(2)}) %collective-permute-start.11) | collective-permute-done | bytes 131104 | tf_op jit(solution)/shard_map/ppermute | solution.py:446
  20.8 3.3 %collective-permute-done.10.refs_6_ = bf16[16,32,128]{2,1,0:T(8,128)(2,1)S(1)} collective-permute-done((bf16[16,32,128]{2,1,0:T(8,128)(2,1)S(1)}, bf16[16,32,128]{2,1,0:T(8,128)(2,1)S(1)}, u32[]{:S(2)}, u32[]{:S(2)}) %collective-permute-start.10) | collective-permute-done | bytes 131104 | tf_op jit(solution)/shard_map/ppermute | solution.py:436
  24.1 0.7 copy-done.1
  24.8 0.9 %select.27 = (bf16[16,64,128]{2,1,0:T(8,128)(2,1)S(1)}, bf16[16,64,128]{2,1,0:T(8,128)(2,1)S(1)}, bf16[16,64,128]{2,1,0:T(8,128)(2,1)S(1)}, bf16[16,64,128]{2,1,0:T(8,128)(2,1)S(1)}) custom-call(s32[1]{0:T(128)} %bitcast.2.me_ref, s32[8,8]{1,0:T(8,128)S(1)} %bitcast.9, s32[8,8]{1,0:T(8,128)S(1)} %collective-permute-done.refs_1_, ...), custom_call_target="tpu_custom_call" | custom-call | bytes 1000000 | tf_op jit(solution)/shard_map/select/pallas_call | solution.py:126
  25.7 0.6 collective-permute-start.12
  26.3 3.0 %collective-permute-start.14 = (bf16[16,64,128]{2,1,0:T(8,128)(2,1)S(1)}, bf16[16,64,128]{2,1,0:T(8,128)(2,1)S(1)}, u32[]{:S(2)}, u32[]{:S(2)}) collective-permute-start(bf16[16,64,128]{2,1,0:T(8,128)(2,1)S(1)} %get-tuple-element.42), channel_id=1, source_target_pairs={{0,12},{4,8},{8,4},{12,0},{16,28},{20,24},{24,20},{28,16},{1,13},{... | collective-permute-start | bytes 786440 | tf_op jit(solution)/shard_map/ppermute | solution.py:436
  29.3 1.3 %collective-permute-start.4 = (bf16[16,24,128]{2,1,0:T(8,128)(2,1)S(1)}, bf16[16,24,128]{2,1,0:T(8,128)(2,1)S(1)}, u32[]{:S(2)}, u32[]{:S(2)}) collective-permute-start(bf16[16,24,128]{2,1,0:T(8,128)(2,1)S(1)} %get-tuple-element.30.refs_4_), channel_id=1, source_target_pairs={{0,16},{4,20},{8,24},{12,28},{16,0},{20,4},{24,8},{28,12},{1,17},{... | collective-permute-start | bytes 294920 | tf_op jit(solution)/shard_map/ppermute | solution.py:436
  30.6 3.7 %lagtable.1 = (bf16[2048,2048]{1,0:T(8,128)(2,1)S(1)}, bf16[2048,1280]{1,0:T(8,128)(2,1)S(1)}) custom-call(f32[2,64,1664]{2,1,0:T(8,128)S(1)} %pad_maximum_fusion.coarse_ref, f32[2,32,1664]{2,1,0:T(8,128)S(1)} %pad_maximum_fusion.1.fine_ref), custom_call_target="tpu_custom_call" | custom-call | flops 20447232 | bytes 13631488 | tf_op jit(solution)/shard_map/lagtable/pallas_call | solution.py:255
  34.4 5.2 %collective-permute-done.4.refs_6_ = bf16[16,24,128]{2,1,0:T(8,128)(2,1)S(1)} collective-permute-done((bf16[16,24,128]{2,1,0:T(8,128)(2,1)S(1)}, bf16[16,24,128]{2,1,0:T(8,128)(2,1)S(1)}, u32[]{:S(2)}, u32[]{:S(2)}) %collective-permute-start.4) | collective-permute-done | bytes 98336 | tf_op jit(solution)/shard_map/ppermute | solution.py:436
  39.5 0.9 %select.26 = (bf16[16,40,128]{2,1,0:T(8,128)(2,1)S(1)}, bf16[16,40,128]{2,1,0:T(8,128)(2,1)S(1)}, bf16[16,40,128]{2,1,0:T(8,128)(2,1)S(1)}, bf16[16,40,128]{2,1,0:T(8,128)(2,1)S(1)}) custom-call(s32[1]{0:T(128)} %bitcast.2.me_ref, s32[8,8]{1,0:T(8,128)S(1)} %bitcast.10, s32[8,8]{1,0:T(8,128)S(1)} %collective-permute-done.refs_1_, ...), custom_call_target="tpu_custom_call" | custom-call | bytes 1000000 | tf_op jit(solution)/shard_map/select/pallas_call | solution.py:126
  40.5 1.6 %collective-permute-start.6 = (bf16[16,40,128]{2,1,0:T(8,128)(2,1)S(1)}, bf16[16,40,128]{2,1,0:T(8,128)(2,1)S(1)}, u32[]{:S(2)}, u32[]{:S(2)}) collective-permute-start(bf16[16,40,128]{2,1,0:T(8,128)(2,1)S(1)} %get-tuple-element.34), channel_id=1, source_target_pairs={{0,4},{4,0},{8,12},{12,8},{16,20},{20,16},{24,28},{28,24},{1,5},{5... | collective-permute-start | bytes 491528 | tf_op jit(solution)/shard_map/ppermute | solution.py:436
  42.1 4.0 %collective-permute-start.7 = (bf16[16,40,128]{2,1,0:T(8,128)(2,1)S(1)}, bf16[16,40,128]{2,1,0:T(8,128)(2,1)S(1)}, u32[]{:S(2)}, u32[]{:S(2)}) collective-permute-start(bf16[16,40,128]{2,1,0:T(8,128)(2,1)S(1)} %get-tuple-element.35), channel_id=1, source_target_pairs={{0,8},{4,12},{8,0},{12,4},{16,24},{20,28},{24,16},{28,20},{1,9},{5... | collective-permute-start | bytes 491528 | tf_op jit(solution)/shard_map/ppermute | solution.py:436
  46.1 8.1 %stack0.1.refs_5_.acc_ref = f32[2048,512]{1,0:T(8,128)S(1)} custom-call(s32[512]{0:T(512)S(1)} %get-tuple-element.53.first_ref, s32[512]{0:T(512)S(1)} %get-tuple-element.54.second_ref, bf16[16,64,128]{2,1,0:T(8,128)(2,1)S(1)} %get-tuple-element.39.refs_0_, bf16[16,64,128]{2,1,0:T(8,128)(2,1)S(1)} %collective-permute-done.12.refs_1_, ...), custom_call_target="tpu_custom_call" | custom-call | flops 4294967296 | bytes 12582912 | tf_op jit(solution)/shard_map/stack0/pallas_call | solution.py:298
  54.2 5.5 %stack1.1 = (bf16[2,256,512]{2,1,0:T(8,128)(2,1)}, f32[2,256,512]{2,1,0:T(8,128)S(1)}, bf16[512,1280]{1,0:T(8,128)(2,1)S(1)}) custom-call(s32[1]{0:T(128)} %bitcast.1.core_ref, s32[512]{0:T(512)S(1)} %get-tuple-element.53.first_ref, s32[512]{0:T(512)S(1)} %get-tuple-element.54.second_ref, bf16[16,40,128]{2,1,0:T(8,128)(2,1)S(1)} %get-tuple-element.33.refs_0_, ...), custom_call_target="tpu_custom_call" | custom-call | flops 1342177280 | bytes 6815744 | tf_op jit(solution)/shard_map/stack1/pallas_call | solution.py:359
  59.7 2.2 %stack2.1 = (bf16[2,256,512]{2,1,0:T(8,128)(2,1)}, f32[2,256,512]{2,1,0:T(8,128)S(1)}) custom-call(s32[1]{0:T(128)} %bitcast.1.core_ref, bf16[2048,1280]{1,0:T(8,128)(2,1)S(1)} %get-tuple-element.37.refs_4_.lag_ref, f32[2048,512]{1,0:T(8,128)S(1)} %stack0.1.refs_5_.acc_ref, bf16[512,1280]{1,0:T(8,128)(2,1)S(1)} %get-tuple-element.46.cross), custom_call_target="tpu_custom_call" | custom-call | flops 1342177280 | bytes 6815744 | tf_op jit(solution)/shard_map/stack2/pallas_call | solution.py:374
  61.9 0.5 collective-permute-start.15
  62.4 1.6 %collective-permute-done.17.near_ref.refs_4_ = bf16[2,256,512]{2,1,0:T(8,128)(2,1)S(1)} collective-permute-done((bf16[2,256,512]{2,1,0:T(8,128)(2,1)}, bf16[2,256,512]{2,1,0:T(8,128)(2,1)S(1)}, u32[]{:S(2)}, u32[]{:S(2)}) %collective-permute-start.17) | collective-permute-done | bytes 524320 | tf_op jit(solution)/shard_map/ppermute | solution.py:436
  64.1 1.6 %collective-permute-start.18 = (bf16[256,512]{1,0:T(8,128)(2,1)S(1)}, bf16[256,512]{1,0:T(8,128)(2,1)S(1)}, u32[]{:S(2)}, u32[]{:S(2)}) collective-permute-start(bf16[256,512]{1,0:T(8,128)(2,1)S(1)} %away.3), channel_id=1, source_target_pairs={{0,2},{1,3},{2,0},{3,1},{4,6},{5,7},{6,4},{7,5},{8,10},{9,11},{10,... | collective-permute-start | bytes 786440 | tf_op jit(solution)/shard_map/ppermute | solution.py:436
  65.7 0.7 collective-permute-start.16
  66.4 6.9 %collective-permute-done.18.refs_5_ = bf16[256,512]{1,0:T(8,128)(2,1)S(1)} collective-permute-done((bf16[256,512]{1,0:T(8,128)(2,1)S(1)}, bf16[256,512]{1,0:T(8,128)(2,1)S(1)}, u32[]{:S(2)}, u32[]{:S(2)}) %collective-permute-start.18) | collective-permute-done | bytes 262176 | tf_op jit(solution)/shard_map/ppermute | solution.py:436
  73.3 4.8 %collective-permute-done.16.refs_2_ = bf16[256,512]{1,0:T(8,128)(2,1)S(1)} collective-permute-done((bf16[256,512]{1,0:T(8,128)(2,1)S(1)}, bf16[256,512]{1,0:T(8,128)(2,1)S(1)}, u32[]{:S(2)}, u32[]{:S(2)}) %collective-permute-start.16) | collective-permute-done | bytes 262176 | tf_op jit(solution)/shard_map/ppermute | solution.py:436
  78.1 1.2 %result.1 = f32[512,512]{1,0:T(8,128)} custom-call(s32[1]{0:T(128)} %bitcast.place_ref, f32[2,256,512]{2,1,0:T(8,128)S(1)} %get-tuple-element.44.keep_ref.refs_0_, bf16[2,256,512]{2,1,0:T(8,128)(2,1)S(1)} %collective-permute-done.15.near_ref.refs_1_, bf16[256,512]{1,0:T(8,128)(2,1)S(1)} %collective-permute-done.16.refs_2_, ...), custom_call_target="tpu_custom_call" | custom-call | flops 524288 | bytes 2097152 | tf_op jit(solution)/shard_map/result/pallas_call | solution.py:422
  (35 shorter events, 1.0 us)
Async XLA Ops:
  0.0 39.5 %copy-start.2 = (s32[1,8,8]{2,1,0:T(8,128)S(1)}, s32[1,8,8]{2,1,0:T(8,128)}, u32[]{:S(2)}) copy-start(s32[1,8,8]{2,1,0:T(8,128)} %param.5) | copy-start | bytes 772
  0.0 30.6 %copy-start.4 = (s32[512]{0:T(512)S(1)}, s32[512]{0:T(512)}, u32[]{:S(2)}) copy-start(s32[512]{0:T(512)} %param.7) | copy-start | bytes 6148
  0.0 30.6 %copy-start.3 = (s32[512]{0:T(512)S(1)}, s32[512]{0:T(512)}, u32[]{:S(2)}) copy-start(s32[512]{0:T(512)} %param.6) | copy-start | bytes 6148
  0.0 1.2 %copy-start = (f32[16,2,2,3200]{3,2,1,0:T(2,128)S(1)}, f32[16,2,2,3200]{3,2,1,0:T(2,128)}, u32[]{:S(2)}) copy-start(f32[16,2,2,3200]{3,2,1,0:T(2,128)} %raw_ref.1) | copy-start | bytes 2457604
  2.8 10.5 %collective-permute-start.2 = (s32[8,8]{1,0:T(8,128)}, s32[8,8]{1,0:T(8,128)S(1)}, u32[]{:S(2)}, u32[]{:S(2)}) collective-permute-start(s32[8,8]{1,0:T(8,128)} %bitcast.6), channel_id=1, source_target_pairs={{0,12},{4,8},{8,4},{12,0},{16,28},{20,24},{24,20},{28,16},{1,13},{... | collective-permute-start | bytes 776 | tf_op jit(solution)/shard_map/ppermute | solution.py:436
  6.9 6.7 %collective-permute-start.1 = (s32[8,8]{1,0:T(8,128)}, s32[8,8]{1,0:T(8,128)S(1)}, u32[]{:S(2)}, u32[]{:S(2)}) collective-permute-start(s32[8,8]{1,0:T(8,128)} %bitcast.7), channel_id=1, source_target_pairs={{0,8},{4,12},{8,0},{12,4},{16,24},{20,28},{24,16},{28,20},{1,9},{5... | collective-permute-start | bytes 776 | tf_op jit(solution)/shard_map/ppermute | solution.py:436
  7.3 13.5 %collective-permute-start.11 = (bf16[16,32,128]{2,1,0:T(8,128)(2,1)S(1)}, bf16[16,32,128]{2,1,0:T(8,128)(2,1)S(1)}, u32[]{:S(2)}, u32[]{:S(2)}) collective-permute-start(bf16[16,32,128]{2,1,0:T(8,128)(2,1)S(1)} %get-tuple-element.38), channel_id=1, source_target_pairs={{0,17},{1,16},{2,19},{3,18},{4,21},{5,20},{6,23},{7,22},{8,25},{9,... | collective-permute-start | bytes 393224 | tf_op jit(solution)/shard_map/ppermute | solution.py:446
  8.8 12.0 %collective-permute-start.9 = (bf16[16,32,128]{2,1,0:T(8,128)(2,1)S(1)}, bf16[16,32,128]{2,1,0:T(8,128)(2,1)S(1)}, u32[]{:S(2)}, u32[]{:S(2)}) collective-permute-start(bf16[16,32,128]{2,1,0:T(8,128)(2,1)S(1)} %get-tuple-element.38), channel_id=1, source_target_pairs={{0,1},{1,0},{2,3},{3,2},{4,5},{5,4},{6,7},{7,6},{8,9},{9,8},{10,11... | collective-permute-start | bytes 393224 | tf_op jit(solution)/shard_map/ppermute | solution.py:436
  10.0 14.1 %collective-permute-start.10 = (bf16[16,32,128]{2,1,0:T(8,128)(2,1)S(1)}, bf16[16,32,128]{2,1,0:T(8,128)(2,1)S(1)}, u32[]{:S(2)}, u32[]{:S(2)}) collective-permute-start(bf16[16,32,128]{2,1,0:T(8,128)(2,1)S(1)} %get-tuple-element.27.refs_4_), channel_id=1, source_target_pairs={{0,16},{4,20},{8,24},{12,28},{16,0},{20,4},{24,8},{28,12},{1,17},{... | collective-permute-start | bytes 393224 | tf_op jit(solution)/shard_map/ppermute | solution.py:436
  13.3 3.9 %collective-permute-start = (s32[8,8]{1,0:T(8,128)}, s32[8,8]{1,0:T(8,128)S(1)}, u32[]{:S(2)}, u32[]{:S(2)}) collective-permute-start(s32[8,8]{1,0:T(8,128)} %bitcast.8), channel_id=1, source_target_pairs={{0,4},{4,0},{8,12},{12,8},{16,20},{20,16},{24,28},{28,24},{1,5},{5... | collective-permute-start | bytes 776 | tf_op jit(solution)/shard_map/ppermute | solution.py:436
  13.6 15.7 %collective-permute-start.5 = (bf16[16,16,128]{2,1,0:T(8,128)(2,1)S(1)}, bf16[16,16,128]{2,1,0:T(8,128)(2,1)S(1)}, u32[]{:S(2)}, u32[]{:S(2)}) collective-permute-start(bf16[16,16,128]{2,1,0:T(8,128)(2,1)S(1)} %get-tuple-element.32), channel_id=1, source_target_pairs={{0,17},{1,16},{2,19},{3,18},{4,21},{5,20},{6,23},{7,22},{8,25},{9,... | collective-permute-start | bytes 196616 | tf_op jit(solution)/shard_map/ppermute | solution.py:446
  17.2 17.2 %collective-permute-start.3 = (bf16[16,16,128]{2,1,0:T(8,128)(2,1)S(1)}, bf16[16,16,128]{2,1,0:T(8,128)(2,1)S(1)}, u32[]{:S(2)}, u32[]{:S(2)}) collective-permute-start(bf16[16,16,128]{2,1,0:T(8,128)(2,1)S(1)} %get-tuple-element.32), channel_id=1, source_target_pairs={{0,1},{1,0},{2,3},{3,2},{4,5},{5,4},{6,7},{7,6},{8,9},{9,8},{10,11... | collective-permute-start | bytes 196616 | tf_op jit(solution)/shard_map/ppermute | solution.py:436
  24.1 0.7 copy-start.1
  25.7 20.4 %collective-permute-start.12 = (bf16[16,64,128]{2,1,0:T(8,128)(2,1)S(1)}, bf16[16,64,128]{2,1,0:T(8,128)(2,1)S(1)}, u32[]{:S(2)}, u32[]{:S(2)}) collective-permute-start(bf16[16,64,128]{2,1,0:T(8,128)(2,1)S(1)} %get-tuple-element.40), channel_id=1, source_target_pairs={{0,4},{4,0},{8,12},{12,8},{16,20},{20,16},{24,28},{28,24},{1,5},{5... | collective-permute-start | bytes 786440 | tf_op jit(solution)/shard_map/ppermute | solution.py:436
  26.3 19.8 %collective-permute-start.13 = (bf16[16,64,128]{2,1,0:T(8,128)(2,1)S(1)}, bf16[16,64,128]{2,1,0:T(8,128)(2,1)S(1)}, u32[]{:S(2)}, u32[]{:S(2)}) collective-permute-start(bf16[16,64,128]{2,1,0:T(8,128)(2,1)S(1)} %get-tuple-element.41), channel_id=1, source_target_pairs={{0,8},{4,12},{8,0},{12,4},{16,24},{20,28},{24,16},{28,20},{1,9},{5... | collective-permute-start | bytes 786440 | tf_op jit(solution)/shard_map/ppermute | solution.py:436
  26.3 19.8 %collective-permute-start.14 = (bf16[16,64,128]{2,1,0:T(8,128)(2,1)S(1)}, bf16[16,64,128]{2,1,0:T(8,128)(2,1)S(1)}, u32[]{:S(2)}, u32[]{:S(2)}) collective-permute-start(bf16[16,64,128]{2,1,0:T(8,128)(2,1)S(1)} %get-tuple-element.42), channel_id=1, source_target_pairs={{0,12},{4,8},{8,4},{12,0},{16,28},{20,24},{24,20},{28,16},{1,13},{... | collective-permute-start | bytes 786440 | tf_op jit(solution)/shard_map/ppermute | solution.py:436
  29.3 10.2 %collective-permute-start.4 = (bf16[16,24,128]{2,1,0:T(8,128)(2,1)S(1)}, bf16[16,24,128]{2,1,0:T(8,128)(2,1)S(1)}, u32[]{:S(2)}, u32[]{:S(2)}) collective-permute-start(bf16[16,24,128]{2,1,0:T(8,128)(2,1)S(1)} %get-tuple-element.30.refs_4_), channel_id=1, source_target_pairs={{0,16},{4,20},{8,24},{12,28},{16,0},{20,4},{24,8},{28,12},{1,17},{... | collective-permute-start | bytes 294920 | tf_op jit(solution)/shard_map/ppermute | solution.py:436
  40.5 13.7 %collective-permute-start.6 = (bf16[16,40,128]{2,1,0:T(8,128)(2,1)S(1)}, bf16[16,40,128]{2,1,0:T(8,128)(2,1)S(1)}, u32[]{:S(2)}, u32[]{:S(2)}) collective-permute-start(bf16[16,40,128]{2,1,0:T(8,128)(2,1)S(1)} %get-tuple-element.34), channel_id=1, source_target_pairs={{0,4},{4,0},{8,12},{12,8},{16,20},{20,16},{24,28},{28,24},{1,5},{5... | collective-permute-start | bytes 491528 | tf_op jit(solution)/shard_map/ppermute | solution.py:436
  42.1 12.2 %collective-permute-start.7 = (bf16[16,40,128]{2,1,0:T(8,128)(2,1)S(1)}, bf16[16,40,128]{2,1,0:T(8,128)(2,1)S(1)}, u32[]{:S(2)}, u32[]{:S(2)}) collective-permute-start(bf16[16,40,128]{2,1,0:T(8,128)(2,1)S(1)} %get-tuple-element.35), channel_id=1, source_target_pairs={{0,8},{4,12},{8,0},{12,4},{16,24},{20,28},{24,16},{28,20},{1,9},{5... | collective-permute-start | bytes 491528 | tf_op jit(solution)/shard_map/ppermute | solution.py:436
  46.1 8.1 %collective-permute-start.8 = (bf16[16,40,128]{2,1,0:T(8,128)(2,1)S(1)}, bf16[16,40,128]{2,1,0:T(8,128)(2,1)S(1)}, u32[]{:S(2)}, u32[]{:S(2)}) collective-permute-start(bf16[16,40,128]{2,1,0:T(8,128)(2,1)S(1)} %get-tuple-element.36), channel_id=1, source_target_pairs={{0,12},{4,8},{8,4},{12,0},{16,28},{20,24},{24,20},{28,16},{1,13},{... | collective-permute-start | bytes 491528 | tf_op jit(solution)/shard_map/ppermute | solution.py:436
  61.9 2.1 %collective-permute-start.17 = (bf16[2,256,512]{2,1,0:T(8,128)(2,1)}, bf16[2,256,512]{2,1,0:T(8,128)(2,1)S(1)}, u32[]{:S(2)}, u32[]{:S(2)}) collective-permute-start(bf16[2,256,512]{2,1,0:T(8,128)(2,1)} %get-tuple-element.48), channel_id=1, source_target_pairs={{0,1},{1,0},{2,3},{3,2},{4,5},{5,4},{6,7},{7,6},{8,9},{9,8},{10,11... | collective-permute-start | bytes 1572872 | tf_op jit(solution)/shard_map/ppermute | solution.py:436
  61.9 3.8 %collective-permute-start.15 = (bf16[2,256,512]{2,1,0:T(8,128)(2,1)}, bf16[2,256,512]{2,1,0:T(8,128)(2,1)S(1)}, u32[]{:S(2)}, u32[]{:S(2)}) collective-permute-start(bf16[2,256,512]{2,1,0:T(8,128)(2,1)} %get-tuple-element.45), channel_id=1, source_target_pairs={{0,1},{1,0},{2,3},{3,2},{4,5},{5,4},{6,7},{7,6},{8,9},{9,8},{10,11... | collective-permute-start | bytes 1572872 | tf_op jit(solution)/shard_map/ppermute | solution.py:436
  64.1 9.2 %collective-permute-start.18 = (bf16[256,512]{1,0:T(8,128)(2,1)S(1)}, bf16[256,512]{1,0:T(8,128)(2,1)S(1)}, u32[]{:S(2)}, u32[]{:S(2)}) collective-permute-start(bf16[256,512]{1,0:T(8,128)(2,1)S(1)} %away.3), channel_id=1, source_target_pairs={{0,2},{1,3},{2,0},{3,1},{4,6},{5,7},{6,4},{7,5},{8,10},{9,11},{10,... | collective-permute-start | bytes 786440 | tf_op jit(solution)/shard_map/ppermute | solution.py:436
  65.7 12.4 %collective-permute-start.16 = (bf16[256,512]{1,0:T(8,128)(2,1)S(1)}, bf16[256,512]{1,0:T(8,128)(2,1)S(1)}, u32[]{:S(2)}, u32[]{:S(2)}) collective-permute-start(bf16[256,512]{1,0:T(8,128)(2,1)S(1)} %away.2), channel_id=1, source_target_pairs={{0,2},{1,3},{2,0},{3,1},{4,6},{5,7},{6,4},{7,5},{8,10},{9,11},{10,... | collective-permute-start | bytes 786440 | tf_op jit(solution)/shard_map/ppermute | solution.py:436
where the time goes:
time: 79.5 us; the launch traced here: 79.3 us
  waiting for transfers between devices  27.1 us (34%)
  Pallas kernels  24.3 us (31%)
  starting transfers between devices  23 us (29%)
  other arithmetic  2.95 us (4%)
  local copies, waits for them, and re-layouts  1.88 us (2%)
    ppermute x17, waiting for transfers between devices, swap(): lax.ppermute(x, axis, [(i, i ^ mask) for i in range(lax.axis_size(axis))])  23.4 us
    ppermute x17, starting transfers between devices, swap(): lax.ppermute(x, axis, [(i, i ^ mask) for i in range(lax.axis_size(axis))])  19.5 us
    pallas_call x1, Pallas kernels, stack_big(): pl.pallas_call(functools.partial(stack_big_kernel, len(bufs), tile), name...  8.08 us
    pallas_call x1, Pallas kernels, stack_first(): pl.pallas_call(functools.partial(stack_first_kernel, len(bufs)), name='st...  5.52 us
    pallas_call x1, Pallas kernels, lag_table(): pl.pallas_call(table_kernel, name='lagtable', grid=(LAGS // FINE // step,...  3.75 us
    ppermute x2, waiting for transfers between devices, swap_both(): return lax.ppermute(x, ('pairs', 'win'), perm)  3.62 us
    ppermute x2, starting transfers between devices, swap_both(): return lax.ppermute(x, ('pairs', 'win'), perm)  3.44 us
    cos x2, other arithmetic, base(): return jnp.stack([jnp.cos(angles), -jnp.sin(angles)])  2.68 us
  transfers between devices with their start and end apart: 19, of which 7 were waited for; matrix products, arithmetic and copies ran while one was open for 4% of the time, Pallas kernels for 17%

commit v1 on v0

--- a/solution.py
+++ b/solution.py
@@ -28,7 +28,7 @@
     return math.prod(shape) * jnp.dtype(dtype).itemsize
 
 
-def whiten_kernel(core_ref, raw_ref, keep_big, keep_small, give_big, give_small, tmp):
+def whiten_kernel(core_ref, hbm_ref, keep_big, keep_small, give_big, give_small, raw_ref, tmp, sems):
     stations, windows, _, bins = raw_ref.shape
     blocks = bins // LANES
     half = blocks // 2
@@ -66,6 +66,12 @@
         tmp[slot, 114:116, :] = im[0:windows]
         keep_small[s, 16:24, :] = tmp[slot, 112:120, :].astype(jnp.bfloat16)
 
+    step = stations // sems.shape[0]
+    copies = []
+    for k in range(sems.shape[0]):
+        rows = pl.ds(k * step, step)
+        copies.append(pltpu.make_async_copy(hbm_ref.at[rows], raw_ref.at[rows], sems.at[k]))
+        copies[-1].start()
     tmp[...] = jnp.zeros_like(tmp)
 
     def several(i, carry):
@@ -73,7 +79,9 @@
             station(2 * i + slot, slot)
         return carry
 
-    lax.fori_loop(0, stations // 2, several, 0)
+    for k, copy in enumerate(copies):
+        copy.wait()
+        lax.fori_loop(k * step // 2, (k + 1) * step // 2, several, 0)
 
 
 def whiten(core, raw):
@@ -83,10 +91,14 @@
         whiten_kernel,
         name="whiten",
         out_shape=tuple(jax.ShapeDtypeStruct((stations, r, LANES), jnp.bfloat16) for r in rows),
-        in_specs=[SMEM, VMEM],
+        in_specs=[SMEM, pl.BlockSpec(memory_space=pltpu.HBM)],
         out_specs=(VMEM,) * 4,
-        scratch_shapes=[pltpu.VMEM((2, 120, LANES), jnp.float32)],
-        compiler_params=params(2 * size(raw.shape, raw.dtype)),
+        scratch_shapes=[
+            pltpu.VMEM(raw.shape, raw.dtype),
+            pltpu.VMEM((2, 120, LANES), jnp.float32),
+            pltpu.SemaphoreType.DMA((4,)),
+        ],
+        compiler_params=params(size(raw.shape, raw.dtype)),
         cost_estimate=pl.CostEstimate(flops=2_000_000, bytes_accessed=2_000_000, transcendentals=0),
     )(core, raw)
 
@@ -181,13 +193,13 @@
         )
 
 
-def cross_small(first_ref, second_ref, bufs, table, cross, out):
+def cross_small(start, first_ref, second_ref, bufs, table, cross, out):
     pairs = out.shape[0]
     load_table(bufs, table)
 
     def pair(p, carry):
-        i = first_ref[p]
-        j = second_ref[p]
+        i = first_ref[start + p]
+        j = second_ref[start + p]
         re, im = products(table, i, j, 2)
         at = p * SMALL_ROWS
         cross[pl.ds(at, 8), :] = re
@@ -311,75 +323,48 @@
     )(first, second, *bufs, lag_table)
 
 
-def finish(part, core, lag_ref, acc_ref, cross, send_ref, keep_ref):
-    outer, tile, _ = send_ref.shape
-    group_rows = lag_ref.shape[0] // (2 * outer)
+def stack_small_kernel(count, start, core_ref, first_ref, second_ref, *refs):
+    bufs = refs[:count]
+    lag_ref, acc_ref, send_ref, keep_ref, table, rows, cross = refs[count:]
+    cross_small(start, first_ref, second_ref, bufs, table, rows, cross)
+    core = core_ref[0]
+    outer, tile, pairs = send_ref.shape
     for mine in range(2):
         for at in range(outer):
             group = 2 * at + (core if mine else 1 - core)
-            rows = pl.ds(pl.multiple_of(group * group_rows + part * tile, tile), tile)
-            value = acc_ref[rows, :] + dot_nt(lag_ref[rows, :], cross[...])
+            lags = pl.ds(pl.multiple_of(group * tile, tile), tile)
+            value = acc_ref[lags, start : start + pairs] + dot_nt(lag_ref[lags, :], cross[...])
             if mine:
                 keep_ref[at] = value
             else:
                 send_ref[at] = value.astype(send_ref.dtype)
 
 
-def stack_first_kernel(count, core_ref, first_ref, second_ref, *refs):
-    bufs = refs[:count]
-    lag_ref, acc_ref, send_ref, keep_ref, cross, table, rows = refs[count:]
-    cross_small(first_ref, second_ref, bufs, table, rows, cross)
-    finish(0, core_ref[0], lag_ref, acc_ref, cross, send_ref, keep_ref)
-
-
-def stack_next_kernel(part, core_ref, lag_ref, acc_ref, cross, send_ref, keep_ref):
-    finish(part, core_ref[0], lag_ref, acc_ref, cross, send_ref, keep_ref)
-
-
-def stack_outputs(acc, groups, parts):
-    lags, pairs = acc.shape
-    shape = (groups // 2, lags // groups // parts, pairs)
-    return [jax.ShapeDtypeStruct(shape, jnp.bfloat16), jax.ShapeDtypeStruct(shape, jnp.float32)]
-
-
-def stack_cost(lags, depth, pairs, parts):
-    return pl.CostEstimate(
-        flops=2 * lags * depth * pairs // parts,
-        bytes_accessed=(2 * lags * depth + 8 * lags * pairs) // parts,
-        transcendentals=0,
-    )
-
-
-def stack_first(core, first, second, bufs, lag_table, acc, groups, parts):
+def stack_small(core, first, second, bufs, lag_table, acc, groups, part, parts):
     lags, depth = lag_table.shape
-    pairs = acc.shape[1]
+    pairs = acc.shape[1] // parts
     slots = sum(buf.shape[0] for buf in bufs)
     table = ((slots,) + bufs[0].shape[1:], jnp.float32)
     rows = ((pairs * SMALL_ROWS, LANES), jnp.float32)
-    return pl.pallas_call(
-        functools.partial(stack_first_kernel, len(bufs)),
+    cross = ((pairs, depth), jnp.bfloat16)
+    shape = (groups // 2, lags // groups, pairs)
+    return pl.pallas_call(
+        functools.partial(stack_small_kernel, len(bufs), part * pairs),
         name="stack1",
         in_specs=[SMEM] * 3 + [VMEM] * (len(bufs) + 2),
-        out_specs=[VMEM] * 3,
-        scratch_shapes=[pltpu.VMEM(*table), pltpu.VMEM(*rows)],
-        out_shape=stack_outputs(acc, groups, parts)
-        + [jax.ShapeDtypeStruct((pairs, depth), jnp.bfloat16)],
-        compiler_params=params(size(*table), size(*rows), roomy=len(bufs) == 1),
-        cost_estimate=stack_cost(lags, depth, pairs, parts),
+        out_specs=[VMEM] * 2,
+        scratch_shapes=[pltpu.VMEM(*table), pltpu.VMEM(*rows), pltpu.VMEM(*cross)],
+        out_shape=[
+            jax.ShapeDtypeStruct(shape, jnp.bfloat16),
+            jax.ShapeDtypeStruct(shape, jnp.float32),
+        ],
+        compiler_params=params(size(*table), size(*rows), size(*cross), roomy=len(bufs) == 1),
+        cost_estimate=pl.CostEstimate(
+            flops=2 * lags * depth * pairs,
+            bytes_accessed=2 * lags * depth + 8 * lags * pairs,
+            transcendentals=0,
+        ),
     )(core, first, second, *bufs, lag_table, acc)
-
-
-def stack_next(core, lag_table, acc, cross, groups, part, parts):
-    lags, depth = lag_table.shape
-    return pl.pallas_call(
-        functools.partial(stack_next_kernel, part),
-        name="stack2",
-        in_specs=[SMEM] + [VMEM] * 3,
-        out_specs=[VMEM] * 2,
-        out_shape=stack_outputs(acc, groups, parts),
-        compiler_params=params(),
-        cost_estimate=stack_cost(lags, depth, acc.shape[1], parts),
-    )(core, lag_table, acc, cross)
 
 
 def away_kernel(place_ref, keep_ref, near_ref, *outs):
@@ -412,8 +397,8 @@
         total = keep[place] + near[place].astype(jnp.float32)
         for ref in far:
             total = total + ref[...].astype(jnp.float32)
-        lags = total.shape[0]
-        out[part * lags : (part + 1) * lags, :] = scale * total
+        pairs = total.shape[1]
+        out[:, part * pairs : (part + 1) * pairs] = scale * total
 
 
 def result(place, pieces, scale):
@@ -422,10 +407,10 @@
     return pl.pallas_call(
         functools.partial(result_kernel, scale, len(pieces)),
         name="result",
-        out_shape=jax.ShapeDtypeStruct((lags * len(pieces), pairs), jnp.float32),
+        out_shape=jax.ShapeDtypeStruct((lags, pairs * len(pieces)), jnp.float32),
         in_specs=[SMEM] + [VMEM] * len(operands),
         out_specs=VMEM,
-        compiler_params=params(2 * size((lags * len(pieces), pairs), jnp.float32)),
+        compiler_params=params(2 * size((lags, pairs * len(pieces)), jnp.float32)),
         cost_estimate=pl.CostEstimate(
             flops=lags * pairs * 4, bytes_accessed=lags * pairs * 16, transcendentals=0
         ),
@@ -451,7 +436,7 @@
 
 
 def local(spectra, requests, pair_first, pair_second):
-    _, windows, _, bins = spectra.shape
+    stations, windows, _, bins = spectra.shape
     sources = lax.axis_size("pairs")
     groups = lax.axis_size("win")
     cap = requests.shape[2]
@@ -461,6 +446,7 @@
     blocks = bins // LANES
     half = blocks // 2
     assert windows == 2 and blocks == 2 * half + 1 and half == 12 and groups % 2 == 0
+    assert stations % 8 == 0
 
     keep_big, keep_small, give_big, give_small = whiten(core[None], spectra)
     coarse, fine = lag_bases(core, half, blocks)
@@ -478,8 +464,8 @@
         ]
         wanted = after(requests[0], keep_big)
         asked = [wanted] + [swap(wanted, "pairs", d) for d in range(1, far)]
-        keep_small = after(keep_small, coarse)
-        give_small = after(give_small, coarse)
+        keep_small = after(keep_small, big[2], big[3])
+        give_small = after(give_small, big[2], big[3])
         small = [
             keep_small,
             swap(give_small, "win", 1),
@@ -512,12 +498,10 @@
     place = (group >> 1)[None]
     parts = 2
     pieces = []
-    send, keep, cross = stack_first(
-        core[None], first, second, exchange[1], table_small, acc, groups, parts
-    )
     for part in range(parts):
-        if part > 0:
-            send, keep = stack_next(core[None], table_small, acc, cross, groups, part, parts)
+        send, keep = stack_small(
+            core[None], first, second, exchange[1], table_small, acc, groups, part, parts
+        )
         near = swap(send, "win", 1)
         away = sum_away(place, keep, near)
         pieces.append([keep, near] + [swap(x, "win", 2 * (d + 1)) for d, x in enumerate(away)])

time: 79.5 us -> 77.8 us (0.979)
  waiting for transfers between devices: 27.1 us -> 24.5 us
  Pallas kernels: 24.3 us -> 25.9 us
  starting transfers between devices: 23 us -> 22.2 us
    ppermute x17, waiting for transfers between devices: 23.4 us -> 18.2 us  [swap(): lax.ppermute(x, axis, [(i, i ^ mask) for i in range(lax.axis_size(axis))])]
    ppermute x2, starting transfers between devices: 3.44 us -> 0.22 us  [swap_both(): return lax.ppermute(x, ('pairs', 'win'), perm)]
    ppermute x2, waiting for transfers between devices: 3.62 us -> 6.28 us  [swap_both(): return lax.ppermute(x, ('pairs', 'win'), perm)]
    ppermute x17, starting transfers between devices: 19.5 us -> 22 us  [swap(): lax.ppermute(x, axis, [(i, i ^ mask) for i in range(lax.axis_size(axis))])]
    pallas_call x1, Pallas kernels: 1.64 us -> 2.71 us  [whiten(): pl.pallas_call(whiten_kernel, name='whiten', out_shape=tuple((jax.ShapeDt...]
  transfers between devices with their start and end apart: 19 -> 19, of which waited for: 7 -> 9; matrix products, arithmetic and copies ran while one was open for 4% -> 4% of each run, Pallas kernels for 17% -> 22%
where the time goes in v1:
time: 77.8 us; the launch traced here: 77.6 us
  Pallas kernels  25.9 us (33%)
  waiting for transfers between devices  24.5 us (31%)
  starting transfers between devices  22.2 us (29%)
  other arithmetic  2.95 us (4%)
  local copies, waits for them, and re-layouts  1.88 us (2%)
    ppermute x17, starting transfers between devices, swap(): lax.ppermute(x, axis, [(i, i ^ mask) for i in range(lax.axis_size(axis))])  22 us
    ppermute x17, waiting for transfers between devices, swap(): lax.ppermute(x, axis, [(i, i ^ mask) for i in range(lax.axis_size(axis))])  18.2 us
    pallas_call x2, Pallas kernels, stack_small(): pl.pallas_call(functools.partial(stack_small_kernel, len(bufs), part * pa...  8.28 us
    pallas_call x1, Pallas kernels, stack_big(): pl.pallas_call(functools.partial(stack_big_kernel, len(bufs), tile), name...  8.08 us
    ppermute x2, waiting for transfers between devices, swap_both(): return lax.ppermute(x, ('pairs', 'win'), perm)  6.28 us
    pallas_call x1, Pallas kernels, lag_table(): pl.pallas_call(table_kernel, name='lagtable', grid=(LAGS // FINE // step,...  3.75 us
    pallas_call x1, Pallas kernels, whiten(): pl.pallas_call(whiten_kernel, name='whiten', out_shape=tuple((jax.ShapeDt...  2.71 us
    cos x2, other arithmetic, base(): return jnp.stack([jnp.cos(angles), -jnp.sin(angles)])  2.68 us
  transfers between devices with their start and end apart: 19, of which 9 were waited for; matrix products, arithmetic and copies ran while one was open for 4% of the time, Pallas kernels for 22%

profile of v1, /device:TPU:0, one launch (start us, length us, event | category | flops | bytes accessed | tf_op | source)
XLA Modules:
  0.0 77.6 jit_solution(8105544553813255764)
XLA Ops:
  0.0 1.2 %copy-done = f32[16,2,2,3200]{3,2,1,0:T(2,128)S(1)} copy-done((f32[16,2,2,3200]{3,2,1,0:T(2,128)S(1)}, f32[16,2,2,3200]{3,2,1,0:T(2,128)}, u32[]{:S(2)}) %copy-start) | copy-done | bytes 819224
  1.2 2.7 %whiten.1 = (bf16[16,32,128]{2,1,0:T(8,128)(2,1)S(1)}, bf16[16,24,128]{2,1,0:T(8,128)(2,1)S(1)}, bf16[16,32,128]{2,1,0:T(8,128)(2,1)S(1)}, bf16[16,16,128]{2,1,0:T(8,128)(2,1)S(1)}) custom-call(s32[1]{0:T(128)} %bitcast.1.core_ref, f32[16,2,2,3200]{3,2,1,0:T(2,128)S(1)} %copy-done), custom_call_target="tpu_custom_call" | custom-call | flops 2000000 | bytes 2000000 | tf_op jit(solution)/shard_map/whiten/pallas_call | solution.py:90
  3.9 3.0 %collective-permute-start = (s32[8,8]{1,0:T(8,128)}, s32[8,8]{1,0:T(8,128)S(1)}, u32[]{:S(2)}, u32[]{:S(2)}) collective-permute-start(s32[8,8]{1,0:T(8,128)} %bitcast.6), channel_id=1, source_target_pairs={{0,4},{4,0},{8,12},{12,8},{16,20},{20,16},{24,28},{28,24},{1,5},{5... | collective-permute-start | bytes 776 | tf_op jit(solution)/shard_map/ppermute | solution.py:421
  6.9 1.6 %collective-permute-start.1 = (s32[8,8]{1,0:T(8,128)}, s32[8,8]{1,0:T(8,128)S(1)}, u32[]{:S(2)}, u32[]{:S(2)}) collective-permute-start(s32[8,8]{1,0:T(8,128)} %bitcast.7), channel_id=1, source_target_pairs={{0,8},{4,12},{8,0},{12,4},{16,24},{20,28},{24,16},{28,20},{1,9},{5... | collective-permute-start | bytes 776 | tf_op jit(solution)/shard_map/ppermute | solution.py:421
  8.5 2.6 %collective-permute-start.3 = (bf16[16,32,128]{2,1,0:T(8,128)(2,1)S(1)}, bf16[16,32,128]{2,1,0:T(8,128)(2,1)S(1)}, u32[]{:S(2)}, u32[]{:S(2)}) collective-permute-start(bf16[16,32,128]{2,1,0:T(8,128)(2,1)S(1)} %get-tuple-element.26.refs_4_), channel_id=1, source_target_pairs={{0,16},{4,20},{8,24},{12,28},{16,0},{20,4},{24,8},{28,12},{1,17},{... | collective-permute-start | bytes 393224 | tf_op jit(solution)/shard_map/ppermute | solution.py:421
  11.1 0.4 collective-permute-start.11
  11.7 0.9 %fusion.10 = (f32[1,32,1664]{2,1,0:T(8,128)S(1)}, f32[1,32,1664]{2,1,0:T(8,128)S(1)}) fusion(s32[1664]{0:T(1024)S(1)} %add_bitcast_fusion), kind=kLoop, calls=%fused_computation.18 | loop fusion | flops 532480 | bytes 432640 | tf_op jit(solution)/shard_map/cos | solution.py:256
  12.6 1.8 %fusion.4 = (f32[1,64,1664]{2,1,0:T(8,128)S(1)}, f32[1,64,1664]{2,1,0:T(8,128)S(1)}) fusion(s32[1664]{0:T(1024)S(1)} %add_bitcast_fusion, s32[64]{0:T(128)S(1)} %multiply_add_fusion), kind=kLoop, calls=%fused_computation.9 | loop fusion | flops 1064960 | bytes 858880 | tf_op jit(solution)/shard_map/cos | solution.py:256
  14.6 5.0 %collective-permute-done.2.refs_3_ = s32[8,8]{1,0:T(8,128)S(1)} collective-permute-done((s32[8,8]{1,0:T(8,128)}, s32[8,8]{1,0:T(8,128)S(1)}, u32[]{:S(2)}, u32[]{:S(2)}) %collective-permute-start.2) | collective-permute-done | bytes 288 | tf_op jit(solution)/shard_map/ppermute | solution.py:421
  19.6 0.4 collective-permute-done.3.refs_6_
  20.0 2.4 %collective-permute-done.4.refs_7_ = bf16[16,32,128]{2,1,0:T(8,128)(2,1)S(1)} collective-permute-done((bf16[16,32,128]{2,1,0:T(8,128)(2,1)S(1)}, bf16[16,32,128]{2,1,0:T(8,128)(2,1)S(1)}, u32[]{:S(2)}, u32[]{:S(2)}) %collective-permute-start.4) | collective-permute-done | bytes 131104 | tf_op jit(solution)/shard_map/ppermute | solution.py:431
  22.4 0.7 copy-done.1
  23.1 0.9 %select.27 = (bf16[16,64,128]{2,1,0:T(8,128)(2,1)S(1)}, bf16[16,64,128]{2,1,0:T(8,128)(2,1)S(1)}, bf16[16,64,128]{2,1,0:T(8,128)(2,1)S(1)}, bf16[16,64,128]{2,1,0:T(8,128)(2,1)S(1)}) custom-call(s32[1]{0:T(128)} %bitcast.2.me_ref, s32[8,8]{1,0:T(8,128)S(1)} %bitcast.9, s32[8,8]{1,0:T(8,128)S(1)} %collective-permute-done.refs_1_, ...), custom_call_target="tpu_custom_call" | custom-call | bytes 1000000 | tf_op jit(solution)/shard_map/select/pallas_call | solution.py:138
  24.0 0.6 collective-permute-start.12
  24.6 3.0 %collective-permute-start.14 = (bf16[16,64,128]{2,1,0:T(8,128)(2,1)S(1)}, bf16[16,64,128]{2,1,0:T(8,128)(2,1)S(1)}, u32[]{:S(2)}, u32[]{:S(2)}) collective-permute-start(bf16[16,64,128]{2,1,0:T(8,128)(2,1)S(1)} %get-tuple-element.41), channel_id=1, source_target_pairs={{0,12},{4,8},{8,4},{12,0},{16,28},{20,24},{24,20},{28,16},{1,13},{... | collective-permute-start | bytes 786440 | tf_op jit(solution)/shard_map/ppermute | solution.py:421
  27.9 1.0 %collective-permute-done.5.refs_5_ = bf16[16,16,128]{2,1,0:T(8,128)(2,1)S(1)} collective-permute-done((bf16[16,16,128]{2,1,0:T(8,128)(2,1)S(1)}, bf16[16,16,128]{2,1,0:T(8,128)(2,1)S(1)}, u32[]{:S(2)}, u32[]{:S(2)}) %collective-permute-start.5) | collective-permute-done | bytes 65568 | tf_op jit(solution)/shard_map/ppermute | solution.py:421
  28.9 1.9 %collective-permute-start.6 = (bf16[16,24,128]{2,1,0:T(8,128)(2,1)S(1)}, bf16[16,24,128]{2,1,0:T(8,128)(2,1)S(1)}, u32[]{:S(2)}, u32[]{:S(2)}) collective-permute-start(bf16[16,24,128]{2,1,0:T(8,128)(2,1)S(1)} %get-tuple-element.30.refs_4_), channel_id=1, source_target_pairs={{0,16},{4,20},{8,24},{12,28},{16,0},{20,4},{24,8},{28,12},{1,17},{... | collective-permute-start | bytes 294920 | tf_op jit(solution)/shard_map/ppermute | solution.py:421
  30.8 3.7 %lagtable.1 = (bf16[2048,2048]{1,0:T(8,128)(2,1)S(1)}, bf16[2048,1280]{1,0:T(8,128)(2,1)S(1)}) custom-call(f32[2,64,1664]{2,1,0:T(8,128)S(1)} %pad_maximum_fusion.coarse_ref, f32[2,32,1664]{2,1,0:T(8,128)S(1)} %pad_maximum_fusion.1.fine_ref), custom_call_target="tpu_custom_call" | custom-call | flops 20447232 | bytes 13631488 | tf_op jit(solution)/shard_map/lagtable/pallas_call | solution.py:267
  34.5 3.8 %collective-permute-done.7.refs_7_ = bf16[16,16,128]{2,1,0:T(8,128)(2,1)S(1)} collective-permute-done((bf16[16,16,128]{2,1,0:T(8,128)(2,1)S(1)}, bf16[16,16,128]{2,1,0:T(8,128)(2,1)S(1)}, u32[]{:S(2)}, u32[]{:S(2)}) %collective-permute-start.7) | collective-permute-done | bytes 65568 | tf_op jit(solution)/shard_map/ppermute | solution.py:431
  38.4 1.2 %collective-permute-done.6.refs_6_ = bf16[16,24,128]{2,1,0:T(8,128)(2,1)S(1)} collective-permute-done((bf16[16,24,128]{2,1,0:T(8,128)(2,1)S(1)}, bf16[16,24,128]{2,1,0:T(8,128)(2,1)S(1)}, u32[]{:S(2)}, u32[]{:S(2)}) %collective-permute-start.6) | collective-permute-done | bytes 98336 | tf_op jit(solution)/shard_map/ppermute | solution.py:421
  39.6 0.9 %select.26 = (bf16[16,40,128]{2,1,0:T(8,128)(2,1)S(1)}, bf16[16,40,128]{2,1,0:T(8,128)(2,1)S(1)}, bf16[16,40,128]{2,1,0:T(8,128)(2,1)S(1)}, bf16[16,40,128]{2,1,0:T(8,128)(2,1)S(1)}) custom-call(s32[1]{0:T(128)} %bitcast.2.me_ref, s32[8,8]{1,0:T(8,128)S(1)} %bitcast.10, s32[8,8]{1,0:T(8,128)S(1)} %collective-permute-done.refs_1_, ...), custom_call_target="tpu_custom_call" | custom-call | bytes 1000000 | tf_op jit(solution)/shard_map/select/pallas_call | solution.py:138
  40.5 4.4 %collective-permute-start.10 = (bf16[16,40,128]{2,1,0:T(8,128)(2,1)S(1)}, bf16[16,40,128]{2,1,0:T(8,128)(2,1)S(1)}, u32[]{:S(2)}, u32[]{:S(2)}) collective-permute-start(bf16[16,40,128]{2,1,0:T(8,128)(2,1)S(1)} %get-tuple-element.36), channel_id=1, source_target_pairs={{0,12},{4,8},{8,4},{12,0},{16,28},{20,24},{24,20},{28,16},{1,13},{... | collective-permute-start | bytes 491528 | tf_op jit(solution)/shard_map/ppermute | solution.py:421
  44.9 0.6 collective-permute-start.8
  45.6 8.1 %stack0.1.refs_5_ = f32[2048,512]{1,0:T(8,128)S(1)} custom-call(s32[512]{0:T(512)S(1)} %get-tuple-element.51.first_ref, s32[512]{0:T(512)S(1)} %get-tuple-element.52.second_ref, bf16[16,64,128]{2,1,0:T(8,128)(2,1)S(1)} %get-tuple-element.38.refs_0_, bf16[16,64,128]{2,1,0:T(8,128)(2,1)S(1)} %collective-permute-done.12.refs_1_, ...), custom_call_target="tpu_custom_call" | custom-call | flops 4294967296 | bytes 12582912 | tf_op jit(solution)/shard_map/stack0/pallas_call | solution.py:310
  53.7 4.1 %stack1.3 = (bf16[2,512,256]{2,1,0:T(8,128)(2,1)}, f32[2,512,256]{2,1,0:T(8,128)S(1)}) custom-call(s32[1]{0:T(128)} %bitcast.1.core_ref, s32[512]{0:T(512)S(1)} %get-tuple-element.51.first_ref, s32[512]{0:T(512)S(1)} %get-tuple-element.52.second_ref, bf16[16,40,128]{2,1,0:T(8,128)(2,1)S(1)} %get-tuple-element.33.refs_0_, ...), custom_call_target="tpu_custom_call" | custom-call | flops 1342177280 | bytes 9437184 | tf_op jit(solution)/shard_map/stack1/pallas_call | solution.py:351
  57.8 4.1 %stack1.2 = (bf16[2,512,256]{2,1,0:T(8,128)(2,1)}, f32[2,512,256]{2,1,0:T(8,128)S(1)}) custom-call(s32[1]{0:T(128)} %bitcast.1.core_ref, s32[512]{0:T(512)S(1)} %get-tuple-element.51.first_ref, s32[512]{0:T(512)S(1)} %get-tuple-element.52.second_ref, bf16[16,40,128]{2,1,0:T(8,128)(2,1)S(1)} %get-tuple-element.33.refs_0_, ...), custom_call_target="tpu_custom_call" | custom-call | flops 1342177280 | bytes 9437184 | tf_op jit(solution)/shard_map/stack1/pallas_call | solution.py:351
  62.0 0.5 collective-permute-start.15
  62.5 1.6 %collective-permute-start.18 = (bf16[512,256]{1,0:T(8,128)(2,1)S(1)}, bf16[512,256]{1,0:T(8,128)(2,1)S(1)}, u32[]{:S(2)}, u32[]{:S(2)}) collective-permute-start(bf16[512,256]{1,0:T(8,128)(2,1)S(1)} %away.3), channel_id=1, source_target_pairs={{0,2},{1,3},{2,0},{3,1},{4,6},{5,7},{6,4},{7,5},{8,10},{9,11},{10,... | collective-permute-start | bytes 786440 | tf_op jit(solution)/shard_map/ppermute | solution.py:421
  64.3 1.6 %collective-permute-start.16 = (bf16[512,256]{1,0:T(8,128)(2,1)S(1)}, bf16[512,256]{1,0:T(8,128)(2,1)S(1)}, u32[]{:S(2)}, u32[]{:S(2)}) collective-permute-start(bf16[512,256]{1,0:T(8,128)(2,1)S(1)} %away.2), channel_id=1, source_target_pairs={{0,2},{1,3},{2,0},{3,1},{4,6},{5,7},{6,4},{7,5},{8,10},{9,11},{10,... | collective-permute-start | bytes 786440 | tf_op jit(solution)/shard_map/ppermute | solution.py:421
  65.9 5.9 %collective-permute-done.18.refs_5_ = bf16[512,256]{1,0:T(8,128)(2,1)S(1)} collective-permute-done((bf16[512,256]{1,0:T(8,128)(2,1)S(1)}, bf16[512,256]{1,0:T(8,128)(2,1)S(1)}, u32[]{:S(2)}, u32[]{:S(2)}) %collective-permute-start.18) | collective-permute-done | bytes 262176 | tf_op jit(solution)/shard_map/ppermute | solution.py:421
  71.8 4.7 %collective-permute-done.16.refs_2_ = bf16[512,256]{1,0:T(8,128)(2,1)S(1)} collective-permute-done((bf16[512,256]{1,0:T(8,128)(2,1)S(1)}, bf16[512,256]{1,0:T(8,128)(2,1)S(1)}, u32[]{:S(2)}, u32[]{:S(2)}) %collective-permute-start.16) | collective-permute-done | bytes 262176 | tf_op jit(solution)/shard_map/ppermute | solution.py:421
  76.4 1.2 %result.1 = f32[512,512]{1,0:T(8,128)} custom-call(s32[1]{0:T(128)} %bitcast.place_ref, f32[2,512,256]{2,1,0:T(8,128)S(1)} %get-tuple-element.43.keep_ref.refs_0_, bf16[2,512,256]{2,1,0:T(8,128)(2,1)S(1)} %collective-permute-done.15.near_ref.refs_1_, bf16[512,256]{1,0:T(8,128)(2,1)S(1)} %collective-permute-done.16.refs_2_, ...), custom_call_target="tpu_custom_call" | custom-call | flops 524288 | bytes 2097152 | tf_op jit(solution)/shard_map/result/pallas_call | solution.py:407
  (35 shorter events, 0.9 us)
Async XLA Ops:
  0.0 39.6 %copy-start.2 = (s32[1,8,8]{2,1,0:T(8,128)S(1)}, s32[1,8,8]{2,1,0:T(8,128)}, u32[]{:S(2)}) copy-start(s32[1,8,8]{2,1,0:T(8,128)} %param.5) | copy-start | bytes 772
  0.0 30.7 %copy-start.3 = (s32[512]{0:T(512)S(1)}, s32[512]{0:T(512)}, u32[]{:S(2)}) copy-start(s32[512]{0:T(512)} %param.6) | copy-start | bytes 6148
  0.0 30.7 %copy-start.4 = (s32[512]{0:T(512)S(1)}, s32[512]{0:T(512)}, u32[]{:S(2)}) copy-start(s32[512]{0:T(512)} %param.7) | copy-start | bytes 6148
  0.0 1.2 %copy-start = (f32[16,2,2,3200]{3,2,1,0:T(2,128)S(1)}, f32[16,2,2,3200]{3,2,1,0:T(2,128)}, u32[]{:S(2)}) copy-start(f32[16,2,2,3200]{3,2,1,0:T(2,128)} %hbm_ref.1) | copy-start | bytes 2457604
  3.9 10.6 %collective-permute-start = (s32[8,8]{1,0:T(8,128)}, s32[8,8]{1,0:T(8,128)S(1)}, u32[]{:S(2)}, u32[]{:S(2)}) collective-permute-start(s32[8,8]{1,0:T(8,128)} %bitcast.6), channel_id=1, source_target_pairs={{0,4},{4,0},{8,12},{12,8},{16,20},{20,16},{24,28},{28,24},{1,5},{5... | collective-permute-start | bytes 776 | tf_op jit(solution)/shard_map/ppermute | solution.py:421
  6.9 7.7 %collective-permute-start.1 = (s32[8,8]{1,0:T(8,128)}, s32[8,8]{1,0:T(8,128)S(1)}, u32[]{:S(2)}, u32[]{:S(2)}) collective-permute-start(s32[8,8]{1,0:T(8,128)} %bitcast.7), channel_id=1, source_target_pairs={{0,8},{4,12},{8,0},{12,4},{16,24},{20,28},{24,16},{28,20},{1,9},{5... | collective-permute-start | bytes 776 | tf_op jit(solution)/shard_map/ppermute | solution.py:421
  8.5 11.5 %collective-permute-start.3 = (bf16[16,32,128]{2,1,0:T(8,128)(2,1)S(1)}, bf16[16,32,128]{2,1,0:T(8,128)(2,1)S(1)}, u32[]{:S(2)}, u32[]{:S(2)}) collective-permute-start(bf16[16,32,128]{2,1,0:T(8,128)(2,1)S(1)} %get-tuple-element.26.refs_4_), channel_id=1, source_target_pairs={{0,16},{4,20},{8,24},{12,28},{16,0},{20,4},{24,8},{28,12},{1,17},{... | collective-permute-start | bytes 393224 | tf_op jit(solution)/shard_map/ppermute | solution.py:421
  11.1 11.3 %collective-permute-start.4 = (bf16[16,32,128]{2,1,0:T(8,128)(2,1)S(1)}, bf16[16,32,128]{2,1,0:T(8,128)(2,1)S(1)}, u32[]{:S(2)}, u32[]{:S(2)}) collective-permute-start(bf16[16,32,128]{2,1,0:T(8,128)(2,1)S(1)} %get-tuple-element.29), channel_id=1, source_target_pairs={{0,17},{1,16},{2,19},{3,18},{4,21},{5,20},{6,23},{7,22},{8,25},{9,... | collective-permute-start | bytes 393224 | tf_op jit(solution)/shard_map/ppermute | solution.py:431
  11.1 11.3 %collective-permute-start.11 = (bf16[16,32,128]{2,1,0:T(8,128)(2,1)S(1)}, bf16[16,32,128]{2,1,0:T(8,128)(2,1)S(1)}, u32[]{:S(2)}, u32[]{:S(2)}) collective-permute-start(bf16[16,32,128]{2,1,0:T(8,128)(2,1)S(1)} %get-tuple-element.29), channel_id=1, source_target_pairs={{0,1},{1,0},{2,3},{3,2},{4,5},{5,4},{6,7},{7,6},{8,9},{9,8},{10,11... | collective-permute-start | bytes 393224 | tf_op jit(solution)/shard_map/ppermute | solution.py:421
  14.5 5.1 %collective-permute-start.2 = (s32[8,8]{1,0:T(8,128)}, s32[8,8]{1,0:T(8,128)S(1)}, u32[]{:S(2)}, u32[]{:S(2)}) collective-permute-start(s32[8,8]{1,0:T(8,128)} %bitcast.8), channel_id=1, source_target_pairs={{0,12},{4,8},{8,4},{12,0},{16,28},{20,24},{24,20},{28,16},{1,13},{... | collective-permute-start | bytes 776 | tf_op jit(solution)/shard_map/ppermute | solution.py:421
  22.4 0.7 copy-start.1
  24.0 21.4 %collective-permute-start.12 = (bf16[16,64,128]{2,1,0:T(8,128)(2,1)S(1)}, bf16[16,64,128]{2,1,0:T(8,128)(2,1)S(1)}, u32[]{:S(2)}, u32[]{:S(2)}) collective-permute-start(bf16[16,64,128]{2,1,0:T(8,128)(2,1)S(1)} %get-tuple-element.39), channel_id=1, source_target_pairs={{0,4},{4,0},{8,12},{12,8},{16,20},{20,16},{24,28},{28,24},{1,5},{5... | collective-permute-start | bytes 786440 | tf_op jit(solution)/shard_map/ppermute | solution.py:421
  24.6 20.9 %collective-permute-start.13 = (bf16[16,64,128]{2,1,0:T(8,128)(2,1)S(1)}, bf16[16,64,128]{2,1,0:T(8,128)(2,1)S(1)}, u32[]{:S(2)}, u32[]{:S(2)}) collective-permute-start(bf16[16,64,128]{2,1,0:T(8,128)(2,1)S(1)} %get-tuple-element.40), channel_id=1, source_target_pairs={{0,8},{4,12},{8,0},{12,4},{16,24},{20,28},{24,16},{28,20},{1,9},{5... | collective-permute-start | bytes 786440 | tf_op jit(solution)/shard_map/ppermute | solution.py:421
  24.6 20.9 %collective-permute-start.14 = (bf16[16,64,128]{2,1,0:T(8,128)(2,1)S(1)}, bf16[16,64,128]{2,1,0:T(8,128)(2,1)S(1)}, u32[]{:S(2)}, u32[]{:S(2)}) collective-permute-start(bf16[16,64,128]{2,1,0:T(8,128)(2,1)S(1)} %get-tuple-element.41), channel_id=1, source_target_pairs={{0,12},{4,8},{8,4},{12,0},{16,28},{20,24},{24,20},{28,16},{1,13},{... | collective-permute-start | bytes 786440 | tf_op jit(solution)/shard_map/ppermute | solution.py:421
  27.6 1.3 %collective-permute-start.5 = (bf16[16,16,128]{2,1,0:T(8,128)(2,1)S(1)}, bf16[16,16,128]{2,1,0:T(8,128)(2,1)S(1)}, u32[]{:S(2)}, u32[]{:S(2)}) collective-permute-start(bf16[16,16,128]{2,1,0:T(8,128)(2,1)S(1)} %get-tuple-element.32), channel_id=1, source_target_pairs={{0,1},{1,0},{2,3},{3,2},{4,5},{5,4},{6,7},{7,6},{8,9},{9,8},{10,11... | collective-permute-start | bytes 196616 | tf_op jit(solution)/shard_map/ppermute | solution.py:421
  27.6 10.7 %collective-permute-start.7 = (bf16[16,16,128]{2,1,0:T(8,128)(2,1)S(1)}, bf16[16,16,128]{2,1,0:T(8,128)(2,1)S(1)}, u32[]{:S(2)}, u32[]{:S(2)}) collective-permute-start(bf16[16,16,128]{2,1,0:T(8,128)(2,1)S(1)} %get-tuple-element.32), channel_id=1, source_target_pairs={{0,17},{1,16},{2,19},{3,18},{4,21},{5,20},{6,23},{7,22},{8,25},{9,... | collective-permute-start | bytes 196616 | tf_op jit(solution)/shard_map/ppermute | solution.py:431
  28.9 10.7 %collective-permute-start.6 = (bf16[16,24,128]{2,1,0:T(8,128)(2,1)S(1)}, bf16[16,24,128]{2,1,0:T(8,128)(2,1)S(1)}, u32[]{:S(2)}, u32[]{:S(2)}) collective-permute-start(bf16[16,24,128]{2,1,0:T(8,128)(2,1)S(1)} %get-tuple-element.30.refs_4_), channel_id=1, source_target_pairs={{0,16},{4,20},{8,24},{12,28},{16,0},{20,4},{24,8},{28,12},{1,17},{... | collective-permute-start | bytes 294920 | tf_op jit(solution)/shard_map/ppermute | solution.py:421
  40.5 13.1 %collective-permute-start.10 = (bf16[16,40,128]{2,1,0:T(8,128)(2,1)S(1)}, bf16[16,40,128]{2,1,0:T(8,128)(2,1)S(1)}, u32[]{:S(2)}, u32[]{:S(2)}) collective-permute-start(bf16[16,40,128]{2,1,0:T(8,128)(2,1)S(1)} %get-tuple-element.36), channel_id=1, source_target_pairs={{0,12},{4,8},{8,4},{12,0},{16,28},{20,24},{24,20},{28,16},{1,13},{... | collective-permute-start | bytes 491528 | tf_op jit(solution)/shard_map/ppermute | solution.py:421
  44.9 8.8 %collective-permute-start.8 = (bf16[16,40,128]{2,1,0:T(8,128)(2,1)S(1)}, bf16[16,40,128]{2,1,0:T(8,128)(2,1)S(1)}, u32[]{:S(2)}, u32[]{:S(2)}) collective-permute-start(bf16[16,40,128]{2,1,0:T(8,128)(2,1)S(1)} %get-tuple-element.34), channel_id=1, source_target_pairs={{0,4},{4,0},{8,12},{12,8},{16,20},{20,16},{24,28},{28,24},{1,5},{5... | collective-permute-start | bytes 491528 | tf_op jit(solution)/shard_map/ppermute | solution.py:421
  45.5 8.2 %collective-permute-start.9 = (bf16[16,40,128]{2,1,0:T(8,128)(2,1)S(1)}, bf16[16,40,128]{2,1,0:T(8,128)(2,1)S(1)}, u32[]{:S(2)}, u32[]{:S(2)}) collective-permute-start(bf16[16,40,128]{2,1,0:T(8,128)(2,1)S(1)} %get-tuple-element.35), channel_id=1, source_target_pairs={{0,8},{4,12},{8,0},{12,4},{16,24},{20,28},{24,16},{28,20},{1,9},{5... | collective-permute-start | bytes 491528 | tf_op jit(solution)/shard_map/ppermute | solution.py:421
  57.8 4.6 %collective-permute-start.17 = (bf16[2,512,256]{2,1,0:T(8,128)(2,1)}, bf16[2,512,256]{2,1,0:T(8,128)(2,1)S(1)}, u32[]{:S(2)}, u32[]{:S(2)}) collective-permute-start(bf16[2,512,256]{2,1,0:T(8,128)(2,1)} %get-tuple-element.46), channel_id=1, source_target_pairs={{0,1},{1,0},{2,3},{3,2},{4,5},{5,4},{6,7},{7,6},{8,9},{9,8},{10,11... | collective-permute-start | bytes 1572872 | tf_op jit(solution)/shard_map/ppermute | solution.py:421
  62.0 2.3 %collective-permute-start.15 = (bf16[2,512,256]{2,1,0:T(8,128)(2,1)}, bf16[2,512,256]{2,1,0:T(8,128)(2,1)S(1)}, u32[]{:S(2)}, u32[]{:S(2)}) collective-permute-start(bf16[2,512,256]{2,1,0:T(8,128)(2,1)} %get-tuple-element.44), channel_id=1, source_target_pairs={{0,1},{1,0},{2,3},{3,2},{4,5},{5,4},{6,7},{7,6},{8,9},{9,8},{10,11... | collective-permute-start | bytes 1572872 | tf_op jit(solution)/shard_map/ppermute | solution.py:421
  62.5 9.2 %collective-permute-start.18 = (bf16[512,256]{1,0:T(8,128)(2,1)S(1)}, bf16[512,256]{1,0:T(8,128)(2,1)S(1)}, u32[]{:S(2)}, u32[]{:S(2)}) collective-permute-start(bf16[512,256]{1,0:T(8,128)(2,1)S(1)} %away.3), channel_id=1, source_target_pairs={{0,2},{1,3},{2,0},{3,1},{4,6},{5,7},{6,4},{7,5},{8,10},{9,11},{10,... | collective-permute-start | bytes 786440 | tf_op jit(solution)/shard_map/ppermute | solution.py:421
  64.3 12.2 %collective-permute-start.16 = (bf16[512,256]{1,0:T(8,128)(2,1)S(1)}, bf16[512,256]{1,0:T(8,128)(2,1)S(1)}, u32[]{:S(2)}, u32[]{:S(2)}) collective-permute-start(bf16[512,256]{1,0:T(8,128)(2,1)S(1)} %away.2), channel_id=1, source_target_pairs={{0,2},{1,3},{2,0},{3,1},{4,6},{5,7},{6,4},{7,5},{8,10},{9,11},{10,... | collective-permute-start | bytes 786440 | tf_op jit(solution)/shard_map/ppermute | solution.py:421

commit v2 on v1

--- a/solution.py
+++ b/solution.py
@@ -28,7 +28,7 @@
     return math.prod(shape) * jnp.dtype(dtype).itemsize
 
 
-def whiten_kernel(core_ref, hbm_ref, keep_big, keep_small, give_big, give_small, raw_ref, tmp, sems):
+def whiten_kernel(core_ref, raw_ref, keep_big, keep_small, give_big, give_small, tmp):
     stations, windows, _, bins = raw_ref.shape
     blocks = bins // LANES
     half = blocks // 2
@@ -66,12 +66,6 @@
         tmp[slot, 114:116, :] = im[0:windows]
         keep_small[s, 16:24, :] = tmp[slot, 112:120, :].astype(jnp.bfloat16)
 
-    step = stations // sems.shape[0]
-    copies = []
-    for k in range(sems.shape[0]):
-        rows = pl.ds(k * step, step)
-        copies.append(pltpu.make_async_copy(hbm_ref.at[rows], raw_ref.at[rows], sems.at[k]))
-        copies[-1].start()
     tmp[...] = jnp.zeros_like(tmp)
 
     def several(i, carry):
@@ -79,9 +73,7 @@
             station(2 * i + slot, slot)
         return carry
 
-    for k, copy in enumerate(copies):
-        copy.wait()
-        lax.fori_loop(k * step // 2, (k + 1) * step // 2, several, 0)
+    lax.fori_loop(0, stations // 2, several, 0)
 
 
 def whiten(core, raw):
@@ -91,13 +83,9 @@
         whiten_kernel,
         name="whiten",
         out_shape=tuple(jax.ShapeDtypeStruct((stations, r, LANES), jnp.bfloat16) for r in rows),
-        in_specs=[SMEM, pl.BlockSpec(memory_space=pltpu.HBM)],
+        in_specs=[SMEM, VMEM],
         out_specs=(VMEM,) * 4,
-        scratch_shapes=[
-            pltpu.VMEM(raw.shape, raw.dtype),
-            pltpu.VMEM((2, 120, LANES), jnp.float32),
-            pltpu.SemaphoreType.DMA((4,)),
-        ],
+        scratch_shapes=[pltpu.VMEM((2, 120, LANES), jnp.float32)],
         compiler_params=params(size(raw.shape, raw.dtype)),
         cost_estimate=pl.CostEstimate(flops=2_000_000, bytes_accessed=2_000_000, transcendentals=0),
     )(core, raw)
@@ -109,13 +97,13 @@
     return jnp.concatenate([keep, got], axis=1)
 
 
-def select_kernel(peers, sources, cap, small, me_ref, *refs):
+def select_kernel(peers, stages, sources, cap, small, me_ref, *refs):
     asked = refs[:peers]
-    chunks = refs[peers : peers + 4]
-    outs = refs[peers + 4 :]
+    chunks = refs[peers : peers + 2 * stages]
+    outs = refs[peers + 2 * stages :]
     me = me_ref[0]
     for d in range(peers):
-        for h in range(2):
+        for h in range(stages):
             source = me ^ (h * (sources // 2))
             keep, got = chunks[2 * h : 2 * h + 2]
             for c in range(cap):
@@ -132,14 +120,15 @@
 
 def select(me, asked, chunks, cap, small):
     peers = len(asked)
+    stages = len(chunks) // 2
     sources = asked[0].shape[0]
     rows = chunks[0].shape[1] + chunks[1].shape[1]
-    out = jax.ShapeDtypeStruct((2 * cap, rows, LANES), chunks[0].dtype)
-    return pl.pallas_call(
-        functools.partial(select_kernel, peers, sources, cap, small),
+    out = jax.ShapeDtypeStruct((stages * cap, rows, LANES), chunks[0].dtype)
+    return pl.pallas_call(
+        functools.partial(select_kernel, peers, stages, sources, cap, small),
         name="select",
         out_shape=(out,) * peers,
-        in_specs=[SMEM] * (1 + peers) + [VMEM] * 4,
+        in_specs=[SMEM] * (1 + peers) + [VMEM] * len(chunks),
         out_specs=(VMEM,) * peers,
         compiler_params=params(2 * (peers + 2) * size(out.shape, out.dtype)),
         cost_estimate=pl.CostEstimate(flops=0, bytes_accessed=1_000_000, transcendentals=0),
@@ -176,12 +165,12 @@
 SMALL_ROWS = 25
 
 
-def cross_big(first_ref, second_ref, bufs, table, cross, out):
+def cross_big(start, first_ref, second_ref, bufs, table, cross, out):
     pairs = out.shape[0]
     load_table(bufs, table)
 
     def pair(p, carry):
-        re, im = products(table, first_ref[p], second_ref[p], 4)
+        re, im = products(table, first_ref[start + p], second_ref[start + p], 4)
         cross[pl.ds(p * BIG_ROWS, 8), :] = re
         cross[pl.ds(p * BIG_ROWS + 8, 8), :] = im
         return carry
@@ -193,13 +182,13 @@
         )
 
 
-def cross_small(start, first_ref, second_ref, bufs, table, cross, out):
+def cross_small(first_ref, second_ref, bufs, table, cross, out):
     pairs = out.shape[0]
     load_table(bufs, table)
 
     def pair(p, carry):
-        i = first_ref[start + p]
-        j = second_ref[start + p]
+        i = first_ref[p]
+        j = second_ref[p]
         re, im = products(table, i, j, 2)
         at = p * SMALL_ROWS
         cross[pl.ds(at, 8), :] = re
@@ -291,42 +280,54 @@
     return lax.dot_general(a, b, (((1,), (1,)), ((), ())), preferred_element_type=jnp.float32)
 
 
-def stack_big_kernel(count, tile, first_ref, second_ref, *refs):
+def scratch(bufs, pairs, each, depth):
+    slots = sum(buf.shape[0] for buf in bufs)
+    shapes = (
+        ((slots,) + bufs[0].shape[1:], jnp.float32),
+        ((pairs * each, LANES), jnp.float32),
+        ((pairs, depth), jnp.bfloat16),
+    )
+    return dict(
+        scratch_shapes=[pltpu.VMEM(*s) for s in shapes],
+        compiler_params=params(*(size(*s) for s in shapes), roomy=len(bufs) == 1),
+    )
+
+
+def stack_cost(lags, depth, pairs):
+    return pl.CostEstimate(
+        flops=2 * lags * depth * pairs,
+        bytes_accessed=2 * lags * depth + 4 * lags * pairs,
+        transcendentals=0,
+    )
+
+
+def stack_small_kernel(count, tile, first_ref, second_ref, *refs):
     bufs = refs[:count]
     lag_ref, acc_ref, table, rows, cross = refs[count:]
-    cross_big(first_ref, second_ref, bufs, table, rows, cross)
+    cross_small(first_ref, second_ref, bufs, table, rows, cross)
     for t in range(acc_ref.shape[0] // tile):
         at = slice(t * tile, (t + 1) * tile)
         acc_ref[at, :] = dot_nt(lag_ref[at, :], cross[...])
 
 
-def stack_big(first, second, bufs, lag_table, tile):
+def stack_small(first, second, bufs, lag_table, tile):
     lags, depth = lag_table.shape
     pairs = first.shape[0]
-    slots = sum(buf.shape[0] for buf in bufs)
-    table = ((slots,) + bufs[0].shape[1:], jnp.float32)
-    rows = ((pairs * BIG_ROWS, LANES), jnp.float32)
-    cross = ((pairs, depth), jnp.bfloat16)
-    return pl.pallas_call(
-        functools.partial(stack_big_kernel, len(bufs), tile),
+    return pl.pallas_call(
+        functools.partial(stack_small_kernel, len(bufs), tile),
         name="stack0",
         out_shape=jax.ShapeDtypeStruct((lags, pairs), jnp.float32),
         in_specs=[SMEM, SMEM] + [VMEM] * (len(bufs) + 1),
         out_specs=VMEM,
-        scratch_shapes=[pltpu.VMEM(*table), pltpu.VMEM(*rows), pltpu.VMEM(*cross)],
-        compiler_params=params(size(*table), size(*rows), size(*cross), roomy=len(bufs) == 1),
-        cost_estimate=pl.CostEstimate(
-            flops=2 * lags * depth * pairs,
-            bytes_accessed=2 * lags * depth + 4 * lags * pairs,
-            transcendentals=0,
-        ),
+        cost_estimate=stack_cost(lags, depth, pairs),
+        **scratch(bufs, pairs, SMALL_ROWS, depth),
     )(first, second, *bufs, lag_table)
 
 
-def stack_small_kernel(count, start, core_ref, first_ref, second_ref, *refs):
+def stack_big_kernel(count, start, core_ref, first_ref, second_ref, *refs):
     bufs = refs[:count]
     lag_ref, acc_ref, send_ref, keep_ref, table, rows, cross = refs[count:]
-    cross_small(start, first_ref, second_ref, bufs, table, rows, cross)
+    cross_big(start, first_ref, second_ref, bufs, table, rows, cross)
     core = core_ref[0]
     outer, tile, pairs = send_ref.shape
     for mine in range(2):
@@ -340,30 +341,21 @@
                 send_ref[at] = value.astype(send_ref.dtype)
 
 
-def stack_small(core, first, second, bufs, lag_table, acc, groups, part, parts):
+def stack_big(core, first, second, bufs, lag_table, acc, groups, part, parts):
     lags, depth = lag_table.shape
     pairs = acc.shape[1] // parts
-    slots = sum(buf.shape[0] for buf in bufs)
-    table = ((slots,) + bufs[0].shape[1:], jnp.float32)
-    rows = ((pairs * SMALL_ROWS, LANES), jnp.float32)
-    cross = ((pairs, depth), jnp.bfloat16)
     shape = (groups // 2, lags // groups, pairs)
     return pl.pallas_call(
-        functools.partial(stack_small_kernel, len(bufs), part * pairs),
+        functools.partial(stack_big_kernel, len(bufs), part * pairs),
         name="stack1",
         in_specs=[SMEM] * 3 + [VMEM] * (len(bufs) + 2),
         out_specs=[VMEM] * 2,
-        scratch_shapes=[pltpu.VMEM(*table), pltpu.VMEM(*rows), pltpu.VMEM(*cross)],
         out_shape=[
             jax.ShapeDtypeStruct(shape, jnp.bfloat16),
             jax.ShapeDtypeStruct(shape, jnp.float32),
         ],
-        compiler_params=params(size(*table), size(*rows), size(*cross), roomy=len(bufs) == 1),
-        cost_estimate=pl.CostEstimate(
-            flops=2 * lags * depth * pairs,
-            bytes_accessed=2 * lags * depth + 8 * lags * pairs,
-            transcendentals=0,
-        ),
+        cost_estimate=stack_cost(lags, depth, pairs),
+        **scratch(bufs, pairs, BIG_ROWS, depth),
     )(core, first, second, *bufs, lag_table, acc)
 
 
@@ -446,62 +438,63 @@
     blocks = bins // LANES
     half = blocks // 2
     assert windows == 2 and blocks == 2 * half + 1 and half == 12 and groups % 2 == 0
-    assert stations % 8 == 0
+    assert stations % 2 == 0
 
     keep_big, keep_small, give_big, give_small = whiten(core[None], spectra)
-    coarse, fine = lag_bases(core, half, blocks)
-    table_big, table_small = lag_table(coarse, fine)
+    near_big = swap(give_big, "win", 1)
+    near_small = swap(give_small, "win", 1)
 
     slots = sources * cap
-    exchange = []
+    wanted = requests[0]
     if two_stage(sources):
         far = sources // 2
-        big = [
-            keep_big,
-            swap(give_big, "win", 1),
-            swap(keep_big, "pairs", far),
-            swap_both(give_big, far, 1),
-        ]
-        wanted = after(requests[0], keep_big)
-        asked = [wanted] + [swap(wanted, "pairs", d) for d in range(1, far)]
-        keep_small = after(keep_small, big[2], big[3])
-        give_small = after(give_small, big[2], big[3])
-        small = [
-            keep_small,
-            swap(give_small, "win", 1),
-            swap(keep_small, "pairs", far),
-            swap_both(give_small, far, 1),
-        ]
-        for chunks, name in ((big, "big"), (small, "small")):
-            outs = select(me[None], asked, chunks, cap, name == "small")
-            exchange.append([outs[0]] + [swap(outs[d], "pairs", d) for d in range(1, far)])
-
-        def row_of(slot):
+        asked = [wanted] + [swap(wanted, "pairs", d) for d in range(1, sources)]
+        outs = select(me[None], asked, (keep_big, near_big), cap, False)
+        big = [outs[0]] + [swap(outs[d], "pairs", d) for d in range(1, sources)]
+        chunks = (
+            keep_small, near_small, swap(keep_small, "pairs", far), swap_both(give_small, far, 1)
+        )
+        core_table = after(core, outs[0])
+        outs = select(me[None], asked[:far], chunks, cap, True)
+        small = [outs[0]] + [swap(outs[d], "pairs", d) for d in range(1, far)]
+
+        def row_of_big(slot):
+            return ((slot // cap) ^ me) * cap + slot % cap
+
+        def row_of_small(slot):
             apart = (slot // cap) ^ me
             return (apart % far) * (2 * cap) + (apart // far) * cap + slot % cap
 
     else:
-        asked_rows = lax.all_to_all(requests[0], "pairs", split_axis=0, concat_axis=0, tiled=True)
-        for i, (keep, give) in enumerate(((keep_big, give_big), (keep_small, give_small))):
-            chunk = join(keep, swap(give, "win", 1), i == 1)
+        asked_rows = lax.all_to_all(wanted, "pairs", split_axis=0, concat_axis=0, tiled=True)
+
+        def exchange(chunk):
             outgoing = chunk[jnp.maximum(asked_rows, 0)]
             arrived = lax.all_to_all(outgoing, "pairs", split_axis=0, concat_axis=0, tiled=True)
-            exchange.append([arrived.reshape((slots,) + chunk.shape[1:])])
-
-        def row_of(slot):
+            return [arrived.reshape((slots,) + chunk.shape[1:])]
+
+        big = exchange(join(keep_big, near_big, False))
+        small = exchange(join(keep_small, near_small, True))
+        core_table = core
+
+        def row_of_big(slot):
             return slot
 
-    first = row_of(pair_first)
-    second = row_of(pair_second)
-    acc = stack_big(first, second, exchange[0], table_big, LAGS // groups)
+        row_of_small = row_of_big
+
+    coarse, fine = lag_bases(core_table, half, blocks)
+    table_big, table_small = lag_table(coarse, fine)
+    acc = stack_small(
+        row_of_small(pair_first), row_of_small(pair_second), small, table_small, LAGS // groups
+    )
 
     place = (group >> 1)[None]
     parts = 2
+    first = row_of_big(pair_first)
+    second = row_of_big(pair_second)
     pieces = []
     for part in range(parts):
-        send, keep = stack_small(
-            core[None], first, second, exchange[1], table_small, acc, groups, part, parts
-        )
+        send, keep = stack_big(core[None], first, second, big, table_big, acc, groups, part, parts)
         near = swap(send, "win", 1)
         away = sum_away(place, keep, near)
         pieces.append([keep, near] + [swap(x, "win", 2 * (d + 1)) for d, x in enumerate(away)])
@@ -513,10 +506,14 @@
 
 
 def solution(mesh):
-    return jax.shard_map(
+    step = jax.shard_map(
         local,
         mesh=mesh,
         in_specs=(P("pairs", "win", None, None), P("pairs", None, None), P("pairs"), P("pairs")),
         out_specs=P("win", "pairs"),
         check_vma=False,
     )
+    sources = mesh.shape["pairs"]
+    if not two_stage(sources):
+        return step
+    return step

time: 77.8 us -> 86.5 us (1.11)
  the two profiles are of different devices: /device:TPU:0 before, /device:TPU:8 now
where the time goes in v2:
time: 86.5 us; the launch traced here: 86.3 us
  starting transfers between devices  33.1 us (38%)
  Pallas kernels  23.7 us (27%)
  waiting for transfers between devices  23.1 us (27%)
  other arithmetic  3.66 us (4%)
  local copies, waits for them, and re-layouts  2.55 us (3%)
    ppermute x24, starting transfers between devices, swap(): lax.ppermute(x, axis, [(i, i ^ mask) for i in range(lax.axis_size(axis))])  31.8 us
    ppermute x24, waiting for transfers between devices, swap(): lax.ppermute(x, axis, [(i, i ^ mask) for i in range(lax.axis_size(axis))])  22.7 us
    pallas_call x2, Pallas kernels, stack_big(): pl.pallas_call(functools.partial(stack_big_kernel, len(bufs), part * pair...  9 us
    pallas_call x1, Pallas kernels, stack_small(): pl.pallas_call(functools.partial(stack_small_kernel, len(bufs), tile), na...  5.95 us
    pallas_call x1, Pallas kernels, lag_table(): pl.pallas_call(table_kernel, name='lagtable', grid=(LAGS // FINE // step,...  3.75 us
    cos x2, other arithmetic, base(): return jnp.stack([jnp.cos(angles), -jnp.sin(angles)])  2.68 us
    unnamed x6, local copies, waits for them, and re-layouts  2.55 us
    pallas_call x2, Pallas kernels, select(): pl.pallas_call(functools.partial(select_kernel, peers, stages, sources, c...  2.12 us
  transfers between devices with their start and end apart: 25, of which 8 were waited for; matrix products, arithmetic and copies ran while one was open for 4% of the time, Pallas kernels for 21%

profile of v2, /device:TPU:8, one launch (start us, length us, event | category | flops | bytes accessed | tf_op | source)
XLA Modules:
  0.0 86.3 jit_solution(6100132490795875190)
XLA Ops:
  0.0 1.4 %collective-permute-start.2 = (s32[8,8]{1,0:T(8,128)}, s32[8,8]{1,0:T(8,128)S(1)}, u32[]{:S(2)}, u32[]{:S(2)}) collective-permute-start(s32[8,8]{1,0:T(8,128)} %bitcast.6), channel_id=1, source_target_pairs={{0,12},{4,8},{8,4},{12,0},{16,28},{20,24},{24,20},{28,16},{1,13},{... | collective-permute-start | bytes 776 | tf_op jit(solution)/shard_map/ppermute | solution.py:413
  1.4 1.6 %collective-permute-start.1 = (s32[8,8]{1,0:T(8,128)}, s32[8,8]{1,0:T(8,128)S(1)}, u32[]{:S(2)}, u32[]{:S(2)}) collective-permute-start(s32[8,8]{1,0:T(8,128)} %bitcast.7), channel_id=1, source_target_pairs={{0,8},{4,12},{8,0},{12,4},{16,24},{20,28},{24,16},{28,20},{1,9},{5... | collective-permute-start | bytes 776 | tf_op jit(solution)/shard_map/ppermute | solution.py:413
  3.5 1.1 %copy-done = f32[16,2,2,3200]{3,2,1,0:T(2,128)S(1)} copy-done((f32[16,2,2,3200]{3,2,1,0:T(2,128)S(1)}, f32[16,2,2,3200]{3,2,1,0:T(2,128)}, u32[]{:S(2)}) %copy-start) | copy-done | bytes 819224
  4.6 1.6 %whiten.1 = (bf16[16,32,128]{2,1,0:T(8,128)(2,1)S(1)}, bf16[16,24,128]{2,1,0:T(8,128)(2,1)S(1)}, bf16[16,32,128]{2,1,0:T(8,128)(2,1)S(1)}, bf16[16,16,128]{2,1,0:T(8,128)(2,1)S(1)}) custom-call(s32[1]{0:T(128)} %bitcast.1.core_ref, f32[16,2,2,3200]{3,2,1,0:T(2,128)S(1)} %copy-done), custom_call_target="tpu_custom_call" | custom-call | flops 2000000 | bytes 2000000 | tf_op jit(solution)/shard_map/whiten/pallas_call | solution.py:82
  6.3 1.3 %collective-permute-start.17 = (bf16[16,16,128]{2,1,0:T(8,128)(2,1)S(1)}, bf16[16,16,128]{2,1,0:T(8,128)(2,1)S(1)}, u32[]{:S(2)}, u32[]{:S(2)}) collective-permute-start(bf16[16,16,128]{2,1,0:T(8,128)(2,1)S(1)} %get-tuple-element.41), channel_id=1, source_target_pairs={{0,17},{1,16},{2,19},{3,18},{4,21},{5,20},{6,23},{7,22},{8,25},{9,... | collective-permute-start | bytes 196616 | tf_op jit(solution)/shard_map/ppermute | solution.py:423
  7.5 1.5 %collective-permute-start.7 = (bf16[16,32,128]{2,1,0:T(8,128)(2,1)S(1)}, bf16[16,32,128]{2,1,0:T(8,128)(2,1)S(1)}, u32[]{:S(2)}, u32[]{:S(2)}) collective-permute-start(bf16[16,32,128]{2,1,0:T(8,128)(2,1)S(1)} %get-tuple-element.29), channel_id=1, source_target_pairs={{0,1},{1,0},{2,3},{3,2},{4,5},{5,4},{6,7},{7,6},{8,9},{9,8},{10,11... | collective-permute-start | bytes 393224 | tf_op jit(solution)/shard_map/ppermute | solution.py:413
  10.3 2.5 %collective-permute-start.6 = (s32[8,8]{1,0:T(8,128)}, s32[8,8]{1,0:T(8,128)S(1)}, u32[]{:S(2)}, u32[]{:S(2)}) collective-permute-start(s32[8,8]{1,0:T(8,128)} %bitcast.9), channel_id=1, source_target_pairs={{0,28},{4,24},{8,20},{12,16},{16,12},{20,8},{24,4},{28,0},{1,29},{... | collective-permute-start | bytes 776 | tf_op jit(solution)/shard_map/ppermute | solution.py:413
  13.3 4.6 %collective-permute-start.4 = (s32[8,8]{1,0:T(8,128)}, s32[8,8]{1,0:T(8,128)S(1)}, u32[]{:S(2)}, u32[]{:S(2)}) collective-permute-start(s32[8,8]{1,0:T(8,128)} %bitcast.11), channel_id=1, source_target_pairs={{0,20},{4,16},{8,28},{12,24},{16,4},{20,0},{24,12},{28,8},{1,21},{... | collective-permute-start | bytes 776 | tf_op jit(solution)/shard_map/ppermute | solution.py:413
  17.9 1.0 %collective-permute-start.3 = (s32[8,8]{1,0:T(8,128)}, s32[8,8]{1,0:T(8,128)S(1)}, u32[]{:S(2)}, u32[]{:S(2)}) collective-permute-start(s32[8,8]{1,0:T(8,128)} %bitcast.12), channel_id=1, source_target_pairs={{0,16},{4,20},{8,24},{12,28},{16,0},{20,4},{24,8},{28,12},{1,17},{... | collective-permute-start | bytes 776 | tf_op jit(solution)/shard_map/ppermute | solution.py:413
  19.6 0.9 %select.27 = (bf16[16,40,128]{2,1,0:T(8,128)(2,1)S(1)}, bf16[16,40,128]{2,1,0:T(8,128)(2,1)S(1)}, bf16[16,40,128]{2,1,0:T(8,128)(2,1)S(1)}, bf16[16,40,128]{2,1,0:T(8,128)(2,1)S(1)}) custom-call(s32[1]{0:T(128)} %bitcast.2.me_ref, s32[8,8]{1,0:T(8,128)S(1)} %bitcast.13, s32[8,8]{1,0:T(8,128)S(1)} %collective-permute-done.refs_1_, ...), custom_call_target="tpu_custom_call" | custom-call | bytes 1000000 | tf_op jit(solution)/shard_map/select/pallas_call | solution.py:127
  20.5 1.6 %collective-permute-start.18 = (bf16[16,40,128]{2,1,0:T(8,128)(2,1)S(1)}, bf16[16,40,128]{2,1,0:T(8,128)(2,1)S(1)}, u32[]{:S(2)}, u32[]{:S(2)}) collective-permute-start(bf16[16,40,128]{2,1,0:T(8,128)(2,1)S(1)} %get-tuple-element.43), channel_id=1, source_target_pairs={{0,4},{4,0},{8,12},{12,8},{16,20},{20,16},{24,28},{28,24},{1,5},{5... | collective-permute-start | bytes 491528 | tf_op jit(solution)/shard_map/ppermute | solution.py:413
  22.1 2.4 %collective-permute-start.19 = (bf16[16,40,128]{2,1,0:T(8,128)(2,1)S(1)}, bf16[16,40,128]{2,1,0:T(8,128)(2,1)S(1)}, u32[]{:S(2)}, u32[]{:S(2)}) collective-permute-start(bf16[16,40,128]{2,1,0:T(8,128)(2,1)S(1)} %get-tuple-element.44), channel_id=1, source_target_pairs={{0,8},{4,12},{8,0},{12,4},{16,24},{20,28},{24,16},{28,20},{1,9},{5... | collective-permute-start | bytes 491528 | tf_op jit(solution)/shard_map/ppermute | solution.py:413
  24.5 1.0 %collective-permute-start.20 = (bf16[16,40,128]{2,1,0:T(8,128)(2,1)S(1)}, bf16[16,40,128]{2,1,0:T(8,128)(2,1)S(1)}, u32[]{:S(2)}, u32[]{:S(2)}) collective-permute-start(bf16[16,40,128]{2,1,0:T(8,128)(2,1)S(1)} %get-tuple-element.45), channel_id=1, source_target_pairs={{0,12},{4,8},{8,4},{12,0},{16,28},{20,24},{24,20},{28,16},{1,13},{... | collective-permute-start | bytes 491528 | tf_op jit(solution)/shard_map/ppermute | solution.py:413
  26.2 1.2 %select.26 = (bf16[8,64,128]{2,1,0:T(8,128)(2,1)S(1)}, bf16[8,64,128]{2,1,0:T(8,128)(2,1)S(1)}, bf16[8,64,128]{2,1,0:T(8,128)(2,1)S(1)}, bf16[8,64,128]{2,1,0:T(...) custom-call(s32[1]{0:T(128)} %bitcast.2.me_ref, ...), custom_call_target="tpu_custom_call" | custom-call | bytes 1000000 | tf_op jit(solution)/shard_map/select/pallas_call | solution.py:127
  28.1 2.0 %collective-permute-start.9 = (bf16[8,64,128]{2,1,0:T(8,128)(2,1)S(1)}, bf16[8,64,128]{2,1,0:T(8,128)(2,1)S(1)}, u32[]{:S(2)}, u32[]{:S(2)}) collective-permute-start(bf16[8,64,128]{2,1,0:T(8,128)(2,1)S(1)} %get-tuple-element.32), channel_id=1, source_target_pairs={{0,8},{4,12},{8,0},{12,4},{16,24},{20,28},{24,16},{28,20},{1,9},{5... | collective-permute-start | bytes 393224 | tf_op jit(solution)/shard_map/ppermute | solution.py:413
  31.0 1.8 %fusion.4 = (f32[1,64,1664]{2,1,0:T(8,128)S(1)}, f32[1,64,1664]{2,1,0:T(8,128)S(1)}) fusion(s32[1664]{0:T(1024)S(1)} %add_bitcast_fusion, s32[64]{0:T(128)S(1)} %multiply_add_fusion.2), kind=kLoop, calls=%fused_computation.9 | loop fusion | flops 1064960 | bytes 858880 | tf_op jit(solution)/shard_map/cos | solution.py:245
  32.9 3.7 %lagtable.1 = (bf16[2048,2048]{1,0:T(8,128)(2,1)S(1)}, bf16[2048,1280]{1,0:T(8,128)(2,1)S(1)}) custom-call(f32[2,64,1664]{2,1,0:T(8,128)S(1)} %pad_maximum_fusion.coarse_ref, f32[2,32,1664]{2,1,0:T(8,128)S(1)} %pad_maximum_fusion.1.fine_ref), custom_call_target="tpu_custom_call" | custom-call | flops 20447232 | bytes 13631488 | tf_op jit(solution)/shard_map/lagtable/pallas_call | solution.py:256
  36.6 1.1 %collective-permute-start.10 = (bf16[8,64,128]{2,1,0:T(8,128)(2,1)S(1)}, bf16[8,64,128]{2,1,0:T(8,128)(2,1)S(1)}, u32[]{:S(2)}, u32[]{:S(2)}) collective-permute-start(bf16[8,64,128]{2,1,0:T(8,128)(2,1)S(1)} %get-tuple-element.33), channel_id=1, source_target_pairs={{0,12},{4,8},{8,4},{12,0},{16,28},{20,24},{24,20},{28,16},{1,13},{... | collective-permute-start | bytes 393224 | tf_op jit(solution)/shard_map/ppermute | solution.py:413
  38.2 2.4 %collective-permute-start.12 = (bf16[8,64,128]{2,1,0:T(8,128)(2,1)S(1)}, bf16[8,64,128]{2,1,0:T(8,128)(2,1)S(1)}, u32[]{:S(2)}, u32[]{:S(2)}) collective-permute-start(bf16[8,64,128]{2,1,0:T(8,128)(2,1)S(1)} %get-tuple-element.35), channel_id=1, source_target_pairs={{0,20},{4,16},{8,28},{12,24},{16,4},{20,0},{24,12},{28,8},{1,21},{... | collective-permute-start | bytes 393224 | tf_op jit(solution)/shard_map/ppermute | solution.py:413
  41.4 2.1 %collective-permute-start.14 = (bf16[8,64,128]{2,1,0:T(8,128)(2,1)S(1)}, bf16[8,64,128]{2,1,0:T(8,128)(2,1)S(1)}, u32[]{:S(2)}, u32[]{:S(2)}) collective-permute-start(bf16[8,64,128]{2,1,0:T(8,128)(2,1)S(1)} %get-tuple-element.37), channel_id=1, source_target_pairs={{0,28},{4,24},{8,20},{12,16},{16,12},{20,8},{24,4},{28,0},{1,29},{... | collective-permute-start | bytes 393224 | tf_op jit(solution)/shard_map/ppermute | solution.py:413
  43.6 5.9 %stack0.1.refs_9_ = f32[2048,512]{1,0:T(8,128)S(1)} custom-call(s32[512]{0:T(512)S(1)} %get-tuple-element.57.first_ref, s32[512]{0:T(512)S(1)} %get-tuple-element.60.second_ref, bf16[16,40,128]{2,1,0:T(8,128)(2,1)S(1)} %get-tuple-element.42.refs_0_, bf16[16,40,128]{2,1,0:T(8,128)(2,1)S(1)} %collective-permute-done.18.refs_1_, ...), custom_call_target="tpu_custom_call" | custom-call | flops 2684354560 | bytes 9437184 | tf_op jit(solution)/shard_map/stack0/pallas_call | solution.py:316
  49.5 2.8 %collective-permute-done.11.refs_4_ = bf16[8,64,128]{2,1,0:T(8,128)(2,1)S(1)} collective-permute-done((bf16[8,64,128]{2,1,0:T(8,128)(2,1)S(1)}, bf16[8,64,128]{2,1,0:T(8,128)(2,1)S(1)}, u32[]{:S(2)}, u32[]{:S(2)}) %collective-permute-start.11) | collective-permute-done | bytes 131104 | tf_op jit(solution)/shard_map/ppermute | solution.py:413
  52.4 2.8 %collective-permute-done.12.refs_5_ = bf16[8,64,128]{2,1,0:T(8,128)(2,1)S(1)} collective-permute-done((bf16[8,64,128]{2,1,0:T(8,128)(2,1)S(1)}, bf16[8,64,128]{2,1,0:T(8,128)(2,1)S(1)}, u32[]{:S(2)}, u32[]{:S(2)}) %collective-permute-start.12) | collective-permute-done | bytes 131104 | tf_op jit(solution)/shard_map/ppermute | solution.py:413
  55.2 4.7 %collective-permute-done.13.refs_6_ = bf16[8,64,128]{2,1,0:T(8,128)(2,1)S(1)} collective-permute-done((bf16[8,64,128]{2,1,0:T(8,128)(2,1)S(1)}, bf16[8,64,128]{2,1,0:T(8,128)(2,1)S(1)}, u32[]{:S(2)}, u32[]{:S(2)}) %collective-permute-start.13) | collective-permute-done | bytes 131104 | tf_op jit(solution)/shard_map/ppermute | solution.py:413
  59.9 1.6 %collective-permute-done.14.refs_7_ = bf16[8,64,128]{2,1,0:T(8,128)(2,1)S(1)} collective-permute-done((bf16[8,64,128]{2,1,0:T(8,128)(2,1)S(1)}, bf16[8,64,128]{2,1,0:T(8,128)(2,1)S(1)}, u32[]{:S(2)}, u32[]{:S(2)}) %collective-permute-start.14) | collective-permute-done | bytes 131104 | tf_op jit(solution)/shard_map/ppermute | solution.py:413
  61.5 4.5 %stack1.3 = (bf16[2,512,256]{2,1,0:T(8,128)(2,1)}, f32[2,512,256]{2,1,0:T(8,128)S(1)}) custom-call(s32[1]{0:T(128)} %bitcast.1.core_ref, s32[512]{0:T(512)S(1)} %get-tuple-element.58.first_ref, s32[512]{0:T(512)S(1)} %get-tuple-element.59.second_ref, bf16[8,64,128]{2,1,0:T(8,128)(2,1)S(1)} %get-tuple-element.30.refs_0_, ...), custom_call_target="tpu_custom_call" | custom-call | flops 2147483648 | bytes 10485760 | tf_op jit(solution)/shard_map/stack1/pallas_call | solution.py:348
  66.1 4.5 %stack1.2 = (bf16[2,512,256]{2,1,0:T(8,128)(2,1)}, f32[2,512,256]{2,1,0:T(8,128)S(1)}) custom-call(s32[1]{0:T(128)} %bitcast.1.core_ref, s32[512]{0:T(512)S(1)} %get-tuple-element.58.first_ref, s32[512]{0:T(512)S(1)} %get-tuple-element.59.second_ref, bf16[8,64,128]{2,1,0:T(8,128)(2,1)S(1)} %get-tuple-element.30.refs_0_, ...), custom_call_target="tpu_custom_call" | custom-call | flops 2147483648 | bytes 10485760 | tf_op jit(solution)/shard_map/stack1/pallas_call | solution.py:348
  71.2 1.6 %collective-permute-start.24 = (bf16[512,256]{1,0:T(8,128)(2,1)S(1)}, bf16[512,256]{1,0:T(8,128)(2,1)S(1)}, u32[]{:S(2)}, u32[]{:S(2)}) collective-permute-start(bf16[512,256]{1,0:T(8,128)(2,1)S(1)} %away.3), channel_id=1, source_target_pairs={{0,2},{1,3},{2,0},{3,1},{4,6},{5,7},{6,4},{7,5},{8,10},{9,11},{10,... | collective-permute-start | bytes 786440 | tf_op jit(solution)/shard_map/ppermute | solution.py:413
  72.9 1.6 %collective-permute-start.22 = (bf16[512,256]{1,0:T(8,128)(2,1)S(1)}, bf16[512,256]{1,0:T(8,128)(2,1)S(1)}, u32[]{:S(2)}, u32[]{:S(2)}) collective-permute-start(bf16[512,256]{1,0:T(8,128)(2,1)S(1)} %away.2), channel_id=1, source_target_pairs={{0,2},{1,3},{2,0},{3,1},{4,6},{5,7},{6,4},{7,5},{8,10},{9,11},{10,... | collective-permute-start | bytes 786440 | tf_op jit(solution)/shard_map/ppermute | solution.py:413
  74.5 5.9 %collective-permute-done.24.refs_5_ = bf16[512,256]{1,0:T(8,128)(2,1)S(1)} collective-permute-done((bf16[512,256]{1,0:T(8,128)(2,1)S(1)}, bf16[512,256]{1,0:T(8,128)(2,1)S(1)}, u32[]{:S(2)}, u32[]{:S(2)}) %collective-permute-start.24) | collective-permute-done | bytes 262176 | tf_op jit(solution)/shard_map/ppermute | solution.py:413
  80.4 4.7 %collective-permute-done.22.refs_2_ = bf16[512,256]{1,0:T(8,128)(2,1)S(1)} collective-permute-done((bf16[512,256]{1,0:T(8,128)(2,1)S(1)}, bf16[512,256]{1,0:T(8,128)(2,1)S(1)}, u32[]{:S(2)}, u32[]{:S(2)}) %collective-permute-start.22) | collective-permute-done | bytes 262176 | tf_op jit(solution)/shard_map/ppermute | solution.py:413
  85.1 1.2 %result.1 = f32[512,512]{1,0:T(8,128)} custom-call(s32[1]{0:T(128)} %bitcast.place_ref, f32[2,512,256]{2,1,0:T(8,128)S(1)} %get-tuple-element.47.keep_ref.refs_0_, bf16[2,512,256]{2,1,0:T(8,128)(2,1)S(1)} %collective-permute-done.21.near_ref.refs_1_, bf16[512,256]{1,0:T(8,128)(2,1)S(1)} %collective-permute-done.22.refs_2_, ...), custom_call_target="tpu_custom_call" | custom-call | flops 524288 | bytes 2097152 | tf_op jit(solution)/shard_map/result/pallas_call | solution.py:399
  (43 shorter events, 7.5 us)
Async XLA Ops:
  0.0 9.8 %collective-permute-start.2 = (s32[8,8]{1,0:T(8,128)}, s32[8,8]{1,0:T(8,128)S(1)}, u32[]{:S(2)}, u32[]{:S(2)}) collective-permute-start(s32[8,8]{1,0:T(8,128)} %bitcast.6), channel_id=1, source_target_pairs={{0,12},{4,8},{8,4},{12,0},{16,28},{20,24},{24,20},{28,16},{1,13},{... | collective-permute-start | bytes 776 | tf_op jit(solution)/shard_map/ppermute | solution.py:413
  1.4 8.5 %collective-permute-start.1 = (s32[8,8]{1,0:T(8,128)}, s32[8,8]{1,0:T(8,128)S(1)}, u32[]{:S(2)}, u32[]{:S(2)}) collective-permute-start(s32[8,8]{1,0:T(8,128)} %bitcast.7), channel_id=1, source_target_pairs={{0,8},{4,12},{8,0},{12,4},{16,24},{20,28},{24,16},{28,20},{1,9},{5... | collective-permute-start | bytes 776 | tf_op jit(solution)/shard_map/ppermute | solution.py:413
  3.0 7.4 %collective-permute-start = (s32[8,8]{1,0:T(8,128)}, s32[8,8]{1,0:T(8,128)S(1)}, u32[]{:S(2)}, u32[]{:S(2)}) collective-permute-start(s32[8,8]{1,0:T(8,128)} %bitcast.8), channel_id=1, source_target_pairs={{0,4},{4,0},{8,12},{12,8},{16,20},{20,16},{24,28},{28,24},{1,5},{5... | collective-permute-start | bytes 776 | tf_op jit(solution)/shard_map/ppermute | solution.py:413
  3.5 1.1 %copy-start = (f32[16,2,2,3200]{3,2,1,0:T(2,128)S(1)}, f32[16,2,2,3200]{3,2,1,0:T(2,128)}, u32[]{:S(2)}) copy-start(f32[16,2,2,3200]{3,2,1,0:T(2,128)} %raw_ref.1) | copy-start | bytes 2457604
  6.3 6.9 %collective-permute-start.17 = (bf16[16,16,128]{2,1,0:T(8,128)(2,1)S(1)}, bf16[16,16,128]{2,1,0:T(8,128)(2,1)S(1)}, u32[]{:S(2)}, u32[]{:S(2)}) collective-permute-start(bf16[16,16,128]{2,1,0:T(8,128)(2,1)S(1)} %get-tuple-element.41), channel_id=1, source_target_pairs={{0,17},{1,16},{2,19},{3,18},{4,21},{5,20},{6,23},{7,22},{8,25},{9,... | collective-permute-start | bytes 196616 | tf_op jit(solution)/shard_map/ppermute | solution.py:423
  7.5 18.0 %collective-permute-start.7 = (bf16[16,32,128]{2,1,0:T(8,128)(2,1)S(1)}, bf16[16,32,128]{2,1,0:T(8,128)(2,1)S(1)}, u32[]{:S(2)}, u32[]{:S(2)}) collective-permute-start(bf16[16,32,128]{2,1,0:T(8,128)(2,1)S(1)} %get-tuple-element.29), channel_id=1, source_target_pairs={{0,1},{1,0},{2,3},{3,2},{4,5},{5,4},{6,7},{7,6},{8,9},{9,8},{10,11... | collective-permute-start | bytes 393224 | tf_op jit(solution)/shard_map/ppermute | solution.py:413
  9.8 3.5 %collective-permute-start.15 = (bf16[16,16,128]{2,1,0:T(8,128)(2,1)S(1)}, bf16[16,16,128]{2,1,0:T(8,128)(2,1)S(1)}, u32[]{:S(2)}, u32[]{:S(2)}) collective-permute-start(bf16[16,16,128]{2,1,0:T(8,128)(2,1)S(1)} %get-tuple-element.41), channel_id=1, source_target_pairs={{0,1},{1,0},{2,3},{3,2},{4,5},{5,4},{6,7},{7,6},{8,9},{9,8},{10,11... | collective-permute-start | bytes 196616 | tf_op jit(solution)/shard_map/ppermute | solution.py:413
  9.9 8.0 %collective-permute-start.16 = (bf16[16,24,128]{2,1,0:T(8,128)(2,1)S(1)}, bf16[16,24,128]{2,1,0:T(8,128)(2,1)S(1)}, u32[]{:S(2)}, u32[]{:S(2)}) collective-permute-start(bf16[16,24,128]{2,1,0:T(8,128)(2,1)S(1)} %get-tuple-element.40.refs_4_), channel_id=1, source_target_pairs={{0,16},{4,20},{8,24},{12,28},{16,0},{20,4},{24,8},{28,12},{1,17},{... | collective-permute-start | bytes 294920 | tf_op jit(solution)/shard_map/ppermute | solution.py:413
  10.3 10.2 %collective-permute-start.6 = (s32[8,8]{1,0:T(8,128)}, s32[8,8]{1,0:T(8,128)S(1)}, u32[]{:S(2)}, u32[]{:S(2)}) collective-permute-start(s32[8,8]{1,0:T(8,128)} %bitcast.9), channel_id=1, source_target_pairs={{0,28},{4,24},{8,20},{12,16},{16,12},{20,8},{24,4},{28,0},{1,29},{... | collective-permute-start | bytes 776 | tf_op jit(solution)/shard_map/ppermute | solution.py:413
  13.2 9.0 %collective-permute-start.5 = (s32[8,8]{1,0:T(8,128)}, s32[8,8]{1,0:T(8,128)S(1)}, u32[]{:S(2)}, u32[]{:S(2)}) collective-permute-start(s32[8,8]{1,0:T(8,128)} %bitcast.10), channel_id=1, source_target_pairs={{0,24},{4,28},{8,16},{12,20},{16,8},{20,12},{24,0},{28,4},{1,25},{... | collective-permute-start | bytes 776 | tf_op jit(solution)/shard_map/ppermute | solution.py:413
  13.3 11.2 %collective-permute-start.4 = (s32[8,8]{1,0:T(8,128)}, s32[8,8]{1,0:T(8,128)S(1)}, u32[]{:S(2)}, u32[]{:S(2)}) collective-permute-start(s32[8,8]{1,0:T(8,128)} %bitcast.11), channel_id=1, source_target_pairs={{0,20},{4,16},{8,28},{12,24},{16,4},{20,0},{24,12},{28,8},{1,21},{... | collective-permute-start | bytes 776 | tf_op jit(solution)/shard_map/ppermute | solution.py:413
  17.9 7.7 %collective-permute-start.3 = (s32[8,8]{1,0:T(8,128)}, s32[8,8]{1,0:T(8,128)S(1)}, u32[]{:S(2)}, u32[]{:S(2)}) collective-permute-start(s32[8,8]{1,0:T(8,128)} %bitcast.12), channel_id=1, source_target_pairs={{0,16},{4,20},{8,24},{12,28},{16,0},{20,4},{24,8},{28,12},{1,17},{... | collective-permute-start | bytes 776 | tf_op jit(solution)/shard_map/ppermute | solution.py:413
  18.8 0.7 copy-start.1
  20.5 16.1 %collective-permute-start.18 = (bf16[16,40,128]{2,1,0:T(8,128)(2,1)S(1)}, bf16[16,40,128]{2,1,0:T(8,128)(2,1)S(1)}, u32[]{:S(2)}, u32[]{:S(2)}) collective-permute-start(bf16[16,40,128]{2,1,0:T(8,128)(2,1)S(1)} %get-tuple-element.43), channel_id=1, source_target_pairs={{0,4},{4,0},{8,12},{12,8},{16,20},{20,16},{24,28},{28,24},{1,5},{5... | collective-permute-start | bytes 491528 | tf_op jit(solution)/shard_map/ppermute | solution.py:413
  22.1 15.6 %collective-permute-start.19 = (bf16[16,40,128]{2,1,0:T(8,128)(2,1)S(1)}, bf16[16,40,128]{2,1,0:T(8,128)(2,1)S(1)}, u32[]{:S(2)}, u32[]{:S(2)}) collective-permute-start(bf16[16,40,128]{2,1,0:T(8,128)(2,1)S(1)} %get-tuple-element.44), channel_id=1, source_target_pairs={{0,8},{4,12},{8,0},{12,4},{16,24},{20,28},{24,16},{28,20},{1,9},{5... | collective-permute-start | bytes 491528 | tf_op jit(solution)/shard_map/ppermute | solution.py:413
  24.5 13.7 %collective-permute-start.20 = (bf16[16,40,128]{2,1,0:T(8,128)(2,1)S(1)}, bf16[16,40,128]{2,1,0:T(8,128)(2,1)S(1)}, u32[]{:S(2)}, u32[]{:S(2)}) collective-permute-start(bf16[16,40,128]{2,1,0:T(8,128)(2,1)S(1)} %get-tuple-element.45), channel_id=1, source_target_pairs={{0,12},{4,8},{8,4},{12,0},{16,28},{20,24},{24,20},{28,16},{1,13},{... | collective-permute-start | bytes 491528 | tf_op jit(solution)/shard_map/ppermute | solution.py:413
  25.5 0.7 copy-start.2
  27.6 13.1 %collective-permute-start.8 = (bf16[8,64,128]{2,1,0:T(8,128)(2,1)S(1)}, bf16[8,64,128]{2,1,0:T(8,128)(2,1)S(1)}, u32[]{:S(2)}, u32[]{:S(2)}) collective-permute-start(bf16[8,64,128]{2,1,0:T(8,128)(2,1)S(1)} %get-tuple-element.31), channel_id=1, source_target_pairs={{0,4},{4,0},{8,12},{12,8},{16,20},{20,16},{24,28},{28,24},{1,5},{5... | collective-permute-start | bytes 393224 | tf_op jit(solution)/shard_map/ppermute | solution.py:413
  28.1 13.3 %collective-permute-start.9 = (bf16[8,64,128]{2,1,0:T(8,128)(2,1)S(1)}, bf16[8,64,128]{2,1,0:T(8,128)(2,1)S(1)}, u32[]{:S(2)}, u32[]{:S(2)}) collective-permute-start(bf16[8,64,128]{2,1,0:T(8,128)(2,1)S(1)} %get-tuple-element.32), channel_id=1, source_target_pairs={{0,8},{4,12},{8,0},{12,4},{16,24},{20,28},{24,16},{28,20},{1,9},{5... | collective-permute-start | bytes 393224 | tf_op jit(solution)/shard_map/ppermute | solution.py:413
  36.6 12.9 %collective-permute-start.10 = (bf16[8,64,128]{2,1,0:T(8,128)(2,1)S(1)}, bf16[8,64,128]{2,1,0:T(8,128)(2,1)S(1)}, u32[]{:S(2)}, u32[]{:S(2)}) collective-permute-start(bf16[8,64,128]{2,1,0:T(8,128)(2,1)S(1)} %get-tuple-element.33), channel_id=1, source_target_pairs={{0,12},{4,8},{8,4},{12,0},{16,28},{20,24},{24,20},{28,16},{1,13},{... | collective-permute-start | bytes 393224 | tf_op jit(solution)/shard_map/ppermute | solution.py:413
  37.7 14.7 %collective-permute-start.11 = (bf16[8,64,128]{2,1,0:T(8,128)(2,1)S(1)}, bf16[8,64,128]{2,1,0:T(8,128)(2,1)S(1)}, u32[]{:S(2)}, u32[]{:S(2)}) collective-permute-start(bf16[8,64,128]{2,1,0:T(8,128)(2,1)S(1)} %get-tuple-element.34), channel_id=1, source_target_pairs={{0,16},{4,20},{8,24},{12,28},{16,0},{20,4},{24,8},{28,12},{1,17},{... | collective-permute-start | bytes 393224 | tf_op jit(solution)/shard_map/ppermute | solution.py:413
  38.2 17.0 %collective-permute-start.12 = (bf16[8,64,128]{2,1,0:T(8,128)(2,1)S(1)}, bf16[8,64,128]{2,1,0:T(8,128)(2,1)S(1)}, u32[]{:S(2)}, u32[]{:S(2)}) collective-permute-start(bf16[8,64,128]{2,1,0:T(8,128)(2,1)S(1)} %get-tuple-element.35), channel_id=1, source_target_pairs={{0,20},{4,16},{8,28},{12,24},{16,4},{20,0},{24,12},{28,8},{1,21},{... | collective-permute-start | bytes 393224 | tf_op jit(solution)/shard_map/ppermute | solution.py:413
  40.7 19.2 %collective-permute-start.13 = (bf16[8,64,128]{2,1,0:T(8,128)(2,1)S(1)}, bf16[8,64,128]{2,1,0:T(8,128)(2,1)S(1)}, u32[]{:S(2)}, u32[]{:S(2)}) collective-permute-start(bf16[8,64,128]{2,1,0:T(8,128)(2,1)S(1)} %get-tuple-element.36), channel_id=1, source_target_pairs={{0,24},{4,28},{8,16},{12,20},{16,8},{20,12},{24,0},{28,4},{1,25},{... | collective-permute-start | bytes 393224 | tf_op jit(solution)/shard_map/ppermute | solution.py:413
  41.4 20.1 %collective-permute-start.14 = (bf16[8,64,128]{2,1,0:T(8,128)(2,1)S(1)}, bf16[8,64,128]{2,1,0:T(8,128)(2,1)S(1)}, u32[]{:S(2)}, u32[]{:S(2)}) collective-permute-start(bf16[8,64,128]{2,1,0:T(8,128)(2,1)S(1)} %get-tuple-element.37), channel_id=1, source_target_pairs={{0,28},{4,24},{8,20},{12,16},{16,12},{20,8},{24,4},{28,0},{1,29},{... | collective-permute-start | bytes 393224 | tf_op jit(solution)/shard_map/ppermute | solution.py:413
  66.0 5.1 %collective-permute-start.23 = (bf16[2,512,256]{2,1,0:T(8,128)(2,1)}, bf16[2,512,256]{2,1,0:T(8,128)(2,1)S(1)}, u32[]{:S(2)}, u32[]{:S(2)}) collective-permute-start(bf16[2,512,256]{2,1,0:T(8,128)(2,1)} %get-tuple-element.50), channel_id=1, source_target_pairs={{0,1},{1,0},{2,3},{3,2},{4,5},{5,4},{6,7},{7,6},{8,9},{9,8},{10,11... | collective-permute-start | bytes 1572872 | tf_op jit(solution)/shard_map/ppermute | solution.py:413
  70.6 2.3 %collective-permute-start.21 = (bf16[2,512,256]{2,1,0:T(8,128)(2,1)}, bf16[2,512,256]{2,1,0:T(8,128)(2,1)S(1)}, u32[]{:S(2)}, u32[]{:S(2)}) collective-permute-start(bf16[2,512,256]{2,1,0:T(8,128)(2,1)} %get-tuple-element.48), channel_id=1, source_target_pairs={{0,1},{1,0},{2,3},{3,2},{4,5},{5,4},{6,7},{7,6},{8,9},{9,8},{10,11... | collective-permute-start | bytes 1572872 | tf_op jit(solution)/shard_map/ppermute | solution.py:413
  71.2 9.2 %collective-permute-start.24 = (bf16[512,256]{1,0:T(8,128)(2,1)S(1)}, bf16[512,256]{1,0:T(8,128)(2,1)S(1)}, u32[]{:S(2)}, u32[]{:S(2)}) collective-permute-start(bf16[512,256]{1,0:T(8,128)(2,1)S(1)} %away.3), channel_id=1, source_target_pairs={{0,2},{1,3},{2,0},{3,1},{4,6},{5,7},{6,4},{7,5},{8,10},{9,11},{10,... | collective-permute-start | bytes 786440 | tf_op jit(solution)/shard_map/ppermute | solution.py:413
  72.9 12.2 %collective-permute-start.22 = (bf16[512,256]{1,0:T(8,128)(2,1)S(1)}, bf16[512,256]{1,0:T(8,128)(2,1)S(1)}, u32[]{:S(2)}, u32[]{:S(2)}) collective-permute-start(bf16[512,256]{1,0:T(8,128)(2,1)S(1)} %away.2), channel_id=1, source_target_pairs={{0,2},{1,3},{2,0},{3,1},{4,6},{5,7},{6,4},{7,5},{8,10},{9,11},{10,... | collective-permute-start | bytes 786440 | tf_op jit(solution)/shard_map/ppermute | solution.py:413
